TPU v7x, 256 devices: a whole 4x4x8 slice. The times are simulated.
256 devices in a mesh: fsdp: 64 (over y, z, core), tp: 4 (over x).
Axes of the slice: x: 4, y: 4, z: 8, core: 2. Of those that a mesh axis runs over, the one named last changes fastest.
Arguments:
- grads: float32 [4, 512, 256, 256], P('tp', None, 'fsdp'), may hold values from -200 to 200
- weights: float32 [512, 256, 256], P('tp', 'fsdp'), may hold values from -0.3 to 0.3
- moments: float32 [512, 256, 256], P('tp', 'fsdp'), may hold values from 0.05 to 2
- left_stat: float32 [4, 64, 6, 256, 256], P('tp', 'fsdp'), may hold values from -20 to 200
- right_stat: float32 [4, 64, 6, 256, 256], P('tp', 'fsdp'), may hold values from -20 to 200
- left_root: bfloat16 [4, 64, 6, 256, 256], P('tp', 'fsdp'), may hold values from -1 to 2
- right_root: bfloat16 [4, 64, 6, 256, 256], P('tp', 'fsdp'), may hold values from -1 to 2
- owner: int32 [512], P('tp'), may hold values from 0 to 63, as said below
- extent: int32 [512, 2], P('tp'), may hold values from 1 to 2
Outputs:
- new_weights: float32 [512, 256, 256], P('tp', 'fsdp')
- new_moments: float32 [512, 256, 256], P('tp', 'fsdp')
- new_left: float32 [4, 64, 6, 256, 256], P('tp', 'fsdp')
- new_right: float32 [4, 64, 6, 256, 256], P('tp', 'fsdp')
Inputs may be any that keep to these rules, and one draw needn't show every extreme that they name: `owner`: within each group of 128 consecutive blocks, no device owns more than 6 blocks, and some device owns exactly 6.
All inputs are finite; a program needn't handle non-finite values.
Results may differ from a plain program's by a relative error of at most 0.0003.
Values sent between devices are 32-bit elements; how exact they have to be, the bound alone decides.
A program may use at most 64 MiB of HBM per device.

v0:
```python
import jax
import jax.numpy as jnp
from jax import lax
from jax.sharding import PartitionSpec as P

PRECISE = lax.Precision.HIGHEST
ADAM_BETA = 0.95
STAT_BETA = 0.99
LEARN_RATE = 0.05
ADAM_EPS = 1e-08
NORM_EPS = 1e-06


def extent_mask(extents, row_ids, col_ids, half_size):
    row_live = row_ids[None, :] < extents[:, 0:1] * half_size
    col_live = col_ids[None, :] < extents[:, 1:2] * half_size
    return (row_live[:, :, None] & col_live[:, None, :]).astype(jnp.float32)


def slot_tables(owner_col, owners, load_max):
    column = owner_col.shape[0]
    onehot = (owner_col[:, None] == jnp.arange(owners, dtype=jnp.int32)[None, :]).astype(jnp.int32)
    slot_rank = jnp.sum((jnp.cumsum(onehot, axis=0) - onehot) * onehot, axis=1)
    flat_slot = owner_col * load_max + slot_rank
    slot_hits = flat_slot[:, None] == jnp.arange(owners * load_max, dtype=jnp.int32)[None, :]
    valid_slot = jnp.any(slot_hits, axis=0)
    block_index = jnp.sum(
        jnp.where(slot_hits, jnp.arange(column, dtype=jnp.int32)[:, None], 0), axis=0
    )
    return (flat_slot, valid_slot, block_index)


def refresh(slot_grad, left_old, right_old, left_inv, right_inv, slot_mask):
    left_prod = jnp.einsum("sij,skj->sik", slot_grad, slot_grad, precision=PRECISE)
    right_prod = jnp.einsum("sji,sjk->sik", slot_grad, slot_grad, precision=PRECISE)
    left_new = STAT_BETA * left_old + (1.0 - STAT_BETA) * left_prod
    right_new = STAT_BETA * right_old + (1.0 - STAT_BETA) * right_prod
    inner = jnp.einsum("sij,sjk->sik", left_inv.astype(jnp.float32), slot_grad, precision=PRECISE)
    precond = (
        jnp.einsum("sij,sjk->sik", inner, right_inv.astype(jnp.float32), precision=PRECISE)
        * slot_mask
    )
    return (left_new, right_new, precond)


def on_device(grads, weights, moments, left_stat, right_stat, left_root, right_root, owner, extent):
    owners = lax.axis_size("fsdp")
    my_index = lax.axis_index("fsdp")
    count_blocks, shard_rows, block_size = weights.shape
    load_max = left_stat.shape[2]
    half_size = block_size // 2
    summed = lax.psum_scatter(grads[0], "tp", scatter_dimension=0, tiled=True)
    row_ids = my_index * shard_rows + jnp.arange(shard_rows, dtype=jnp.int32)
    col_ids = jnp.arange(block_size, dtype=jnp.int32)
    summed = summed * extent_mask(extent, row_ids, col_ids, half_size)
    new_moment = ADAM_BETA * moments + (1.0 - ADAM_BETA) * summed * summed
    adam_dir = summed / (jnp.sqrt(new_moment) + ADAM_EPS)
    adam_part = jnp.sum(adam_dir * adam_dir, axis=(1, 2))
    flat_slot, valid_slot, block_index = slot_tables(owner, owners, load_max)
    adam_total = lax.psum(adam_part, "fsdp")
    outgoing = jnp.take(summed, block_index, axis=0) * valid_slot[:, None, None].astype(jnp.float32)
    outgoing = outgoing.reshape(owners, load_max, shard_rows, block_size)
    incoming = lax.all_to_all(outgoing, "fsdp", split_axis=0, concat_axis=2, tiled=True)[0]
    mine_index = lax.dynamic_slice_in_dim(block_index, my_index * load_max, load_max)
    mine_extent = jnp.take(extent, mine_index, axis=0)
    out_mask = extent_mask(mine_extent, col_ids, col_ids, half_size)
    left_new, right_new, precond = refresh(
        incoming, left_stat[0, 0], right_stat[0, 0], left_root[0, 0], right_root[0, 0], out_mask
    )
    prec_owner = jnp.sum(precond * precond, axis=(1, 2))
    spread_sq = jnp.broadcast_to(prec_owner[None, :, None], (1, load_max, owners))
    back_prec, back_sq = (
        lax.all_to_all(precond[None], "fsdp", split_axis=2, concat_axis=0, tiled=True),
        lax.all_to_all(spread_sq, "fsdp", split_axis=2, concat_axis=0, tiled=True),
    )
    home_prec = jnp.take(
        back_prec.reshape(owners * load_max, shard_rows, block_size), flat_slot, axis=0
    )
    prec_total = jnp.take(back_sq.reshape(owners * load_max), flat_slot)
    graft = jnp.sqrt(adam_total / (prec_total + NORM_EPS))
    new_weight = weights - LEARN_RATE * home_prec * graft[:, None, None]
    return (new_weight, new_moment, left_new[None, None], right_new[None, None])


def solution(mesh):
    in_specs = (
        P("tp", None, "fsdp", None),
        P("tp", "fsdp", None),
        P("tp", "fsdp", None),
        P("tp", "fsdp", None, None, None),
        P("tp", "fsdp", None, None, None),
        P("tp", "fsdp", None, None, None),
        P("tp", "fsdp", None, None, None),
        P("tp"),
        P("tp", None),
    )
    out_specs = (
        P("tp", "fsdp", None),
        P("tp", "fsdp", None),
        P("tp", "fsdp", None, None, None),
        P("tp", "fsdp", None, None, None),
    )
    return jax.shard_map(
        on_device, mesh=mesh, in_specs=in_specs, out_specs=out_specs, check_vma=False
    )
```

profile of v0, /device:TPU:1, one launch (start us, length us, event | category | flops | bytes accessed | tf_op | source)
XLA Modules:
  0.0 339.6 jit_solution(3484285128444985306)
XLA Ops:
  7.2 0.0 copy-start
  7.2 0.0 copy-start.7
  7.2 0.0 copy-start.5
  7.2 0.0 copy-start.6
  7.2 0.0 all-reduce.3.cloned.1.call-start
  7.3 0.7 all-reduce.3.cloned.1.call-update
  8.0 0.1 fusion.7
  8.1 0.2 reduce_window_sum.11
  8.2 0.2 select_reduce_fusion.1
  8.4 0.1 fusion.6
  8.6 0.1 reshape.161
  8.7 0.1 select_reduce_fusion
  8.8 0.1 reduce_sum.42
  9.0 0.6 dynamic-slice
  10.3 0.1 broadcast_compare_fusion
  10.4 0.1 iota_compare_fusion.1
  10.5 67.6 %all-reduce.3.cloned.1.call-done = f32[512,4,256]{2,1,0:T(4,128)} async-done(((f32[512,4,256]{2,1,0:T(4,128)}), f32[512,4,256]{2,1,0:T(4,128)}) %all-reduce.3.cloned.1.call-update) | async-done | bytes 2097168
  78.0 3.7 %multiply_reduce_fusion.1 = (f32[128]{0:T(128)S(1)}, f32[128,4,256]{2,1,0:T(4,128)}, f32[128,4,256]{2,1,0:T(4,128)S(1)}) fusion(f32[128,4,256]{2,1,0:T(4,128)S(1)} %copy-done.3, f32[512,4,256]{2,1,0:T(4,128)} %all-reduce.3.cloned.1.call-done, u32[]{:T(128)S(6)} %multiply.3, pred[128,256]{1,0:T(8,128)(4,1)S(1)} %iota_compare_fusion.1, ...), kind=kLoop, calls=%fused_computation.18 | loop fusion | flops 1310592 | bytes 2130948 | tf_op jit(solution)/shard_map/reduce_sum | solution.py:58
  81.7 2.5 gather_fusion.1
  84.2 2.3 select_multiply_fusion
  86.5 10.7 %all-to-all-start = ((f32[64,6,4,256]{3,2,1,0:T(4,128)}), f32[64,6,4,256]{3,2,1,0:T(4,128)S(1)}, u32[]{:S(2)}, u32[]{:S(2)}) async-start(f32[64,6,4,256]{3,2,1,0:T(4,128)} %select_multiply_fusion), calls=%async_computation | async-start | bytes 3145728 | tf_op jit(solution)/shard_map/all_to_all | solution.py:63
  97.2 0.1 copy.52
  97.3 0.1 compare_and_fusion.1
  97.4 0.6 gather_fusion
  97.9 0.1 broadcast_select_fusion
  98.0 0.2 multiply_reduce_fusion.3
  98.2 0.1 iota_compare_fusion.3
  98.3 38.7 %all-to-all-done = f32[64,6,4,256]{3,2,1,0:T(4,128)S(1)} async-done(((f32[64,6,4,256]{3,2,1,0:T(4,128)}), f32[64,6,4,256]{3,2,1,0:T(4,128)S(1)}, u32[]{:S(2)}, u32[]{:S(2)}) %all-to-all-start) | async-done | bytes 1572896 | tf_op jit(solution)/shard_map/all_to_all | solution.py:63
  137.0 1.4 copy.53
  138.4 1.9 squeeze.15
  140.3 1.0 fusion.3
  141.3 2.3 multiply_reduce_fusion
  143.6 0.6 broadcast_in_dim.88
  144.2 6.1 %all-to-all-start.2 = ((f32[1,6,64]{1,0,2:T(1,128)}), f32[1,6,64]{1,0,2:T(1,128)S(1)}, u32[]{:S(2)}, u32[]{:S(2)}) async-start(f32[1,6,64]{1,0,2:T(1,128)} %broadcast_in_dim.88), calls=%async_computation.2 | async-start | bytes 65536 | tf_op jit(solution)/shard_map/all_to_all | solution.py:74
  150.3 4.2 %copy.56 = f32[1,6,256,256]{3,0,1,2:T(1,128)} copy(f32[1,6,256,256]{3,2,1,0:T(8,128)} %bitcast.49) | data formatting | bytes 3145728 | tf_op jit(solution)/shard_map/broadcast_in_dim | solution.py:73
  154.5 5.0 %all-to-all-done.2 = f32[1,6,64]{1,0,2:T(1,128)S(1)} async-done(((f32[1,6,64]{1,0,2:T(1,128)}), f32[1,6,64]{1,0,2:T(1,128)S(1)}, u32[]{:S(2)}, u32[]{:S(2)}) %all-to-all-start.2) | async-done | bytes 1568 | tf_op jit(solution)/shard_map/all_to_all | solution.py:74
  159.5 5.5 %all-to-all-start.1 = ((f32[1,6,256,256]{3,0,1,2:T(1,128)}), f32[1,6,256,256]{3,0,1,2:T(1,128)}, u32[]{:S(2)}, u32[]{:S(2)}) async-start(f32[1,6,256,256]{3,0,1,2:T(1,128)} %copy.56), calls=%async_computation.1 | async-start | bytes 3145728 | tf_op jit(solution)/shard_map/all_to_all | solution.py:73
  165.1 152.9 %psum.7 = f32[128]{0:T(128)S(1)} all-reduce(f32[128]{0:T(128)S(1)} %get-tuple-element.8), channel_id=1, replica_groups=mesh['fsdp'=64,'tp'=4] {'fsdp'}, use_global_device_ids=true, to_apply=%region_6.7 | all-reduce | flops 128 | bytes 1024 | tf_op jit(solution)/shard_map/psum | solution.py:60
  318.0 4.5 %fusion.1 = f32[1,1,6,256,256]{4,3,2,1,0:T(8,128)} fusion(f32[1,1,6,256,256]{4,3,2,1,0:T(8,128)} %param.12, f32[6,256,256]{2,1,0:T(8,128)S(1)} %squeeze.15), kind=kOutput, calls=%fused_computation.7 | convolution fusion | flops 1209139200 | bytes 4718592 | tf_op jit(solution)/shard_map/sij,skj->sik/dot_general | solution.py:34
  322.5 3.9 %fusion = f32[1,1,6,256,256]{4,3,2,1,0:T(8,128)} fusion(f32[1,1,6,256,256]{4,3,2,1,0:T(8,128)S(1)} %copy-done.1, f32[6,256,256]{2,1,0:T(8,128)S(1)} %squeeze.15), kind=kOutput, calls=%fused_computation.5 | convolution fusion | flops 1209139200 | bytes 4718592 | tf_op jit(solution)/shard_map/sji,sjk->sik/dot_general | solution.py:35
  326.4 0.1 reshape.160
  326.5 1.3 gather_fusion.3
  327.8 0.0 all-to-all-done.1
  327.8 2.5 copy.57
  330.3 0.0 copy-start.4
  330.3 0.4 copy.58
  330.8 0.9 gather_fusion.2
  331.7 1.1 multiply_subtract_fusion
  (21 shorter events, 0.1 us)
Async XLA Ops:
  7.2 134.1 %copy-start = (bf16[1,1,6,256,256]{4,3,2,1,0:T(8,128)(2,1)S(1)}, bf16[1,1,6,256,256]{4,3,2,1,0:T(8,128)(2,1)}, u32[]{:S(2)}) copy-start(bf16[1,1,6,256,256]{4,3,2,1,0:T(8,128)(2,1)} %param.15) | copy-start | bytes 2359300
  7.2 1.8 copy-start.7
  7.2 0.8 copy-start.5
  7.2 3.0 copy-start.6
  7.2 70.8 %copy-start.3 = (f32[128,4,256]{2,1,0:T(4,128)S(1)}, f32[128,4,256]{2,1,0:T(4,128)}, u32[]{:S(2)}) copy-start(f32[128,4,256]{2,1,0:T(4,128)} %param.11) | copy-start | bytes 1572868
  7.2 70.8 %all-reduce.3.cloned.1.call-start = ((), (), s32[]{:S(2)}) async-start(), calls=%async_computation.3 | async-start | bytes 4194304
  86.5 50.5 %all-to-all-start = ((f32[64,6,4,256]{3,2,1,0:T(4,128)}), f32[64,6,4,256]{3,2,1,0:T(4,128)S(1)}, u32[]{:S(2)}, u32[]{:S(2)}) async-start(f32[64,6,4,256]{3,2,1,0:T(4,128)} %select_multiply_fusion), calls=%async_computation | async-start | bytes 3145728 | tf_op jit(solution)/shard_map/all_to_all | solution.py:63
  138.4 1.9 copy-start.2
  144.2 15.3 %all-to-all-start.2 = ((f32[1,6,64]{1,0,2:T(1,128)}), f32[1,6,64]{1,0,2:T(1,128)S(1)}, u32[]{:S(2)}, u32[]{:S(2)}) async-start(f32[1,6,64]{1,0,2:T(1,128)} %broadcast_in_dim.88), calls=%async_computation.2 | async-start | bytes 65536 | tf_op jit(solution)/shard_map/all_to_all | solution.py:74
  159.5 168.3 %all-to-all-start.1 = ((f32[1,6,256,256]{3,0,1,2:T(1,128)}), f32[1,6,256,256]{3,0,1,2:T(1,128)}, u32[]{:S(2)}, u32[]{:S(2)}) async-start(f32[1,6,256,256]{3,0,1,2:T(1,128)} %copy.56), calls=%async_computation.1 | async-start | bytes 3145728 | tf_op jit(solution)/shard_map/all_to_all | solution.py:73
  318.0 4.5 %copy-start.1 = (f32[1,1,6,256,256]{4,3,2,1,0:T(8,128)S(1)}, f32[1,1,6,256,256]{4,3,2,1,0:T(8,128)}, u32[]{:S(2)}) copy-start(f32[1,1,6,256,256]{4,3,2,1,0:T(8,128)} %param.13) | copy-start | bytes 4718596
  330.3 1.3 copy-start.4
Sparse Core Ops, SparseCore 0:
  10.4 67.5 all-reduce.2
where the time goes:
time: 340 us
  blocking collectives  153 us (45%)
  waiting for transfers between devices  112 us (33%)
  starting transfers between devices  22.4 us (7%)
  local copies, waits for them, and re-layouts  17.3 us (5%)
  between operations  15 us (4%)
  matrix products  11.6 us (3%)
  other arithmetic  8.41 us (2%)
    psum x1, blocking collectives, on_device(): adam_total = lax.psum(adam_part, 'fsdp')  153 us
    unnamed x2, waiting for transfers between devices  68.2 us
    all_to_all x1, waiting for transfers between devices, on_device(): lax.all_to_all(outgoing, 'fsdp', split_axis=0, concat_axis=2, tiled=True)[0]  38.7 us
    all_to_all x1, starting transfers between devices, on_device(): lax.all_to_all(outgoing, 'fsdp', split_axis=0, concat_axis=2, tiled=True)[0]  10.7 us
  transfers between devices with their start and end apart: 4, of which 3 were waited for; matrix products, arithmetic and copies ran while one was open for 5% of the time, Pallas kernels for 0%

commit v1 on v0

--- a/solution.py
+++ b/solution.py
@@ -49,7 +49,11 @@
     count_blocks, shard_rows, block_size = weights.shape
     load_max = left_stat.shape[2]
     half_size = block_size // 2
-    summed = lax.psum_scatter(grads[0], "tp", scatter_dimension=0, tiled=True)
+    tp_size = lax.axis_size("tp")
+    parts = lax.all_to_all(
+        grads[0].reshape(tp_size, count_blocks, shard_rows, block_size), "tp", split_axis=0, concat_axis=0, tiled=True
+    )
+    summed = jnp.sum(parts, axis=0)
     row_ids = my_index * shard_rows + jnp.arange(shard_rows, dtype=jnp.int32)
     col_ids = jnp.arange(block_size, dtype=jnp.int32)
     summed = summed * extent_mask(extent, row_ids, col_ids, half_size)
@@ -57,7 +61,10 @@
     adam_dir = summed / (jnp.sqrt(new_moment) + ADAM_EPS)
     adam_part = jnp.sum(adam_dir * adam_dir, axis=(1, 2))
     flat_slot, valid_slot, block_index = slot_tables(owner, owners, load_max)
-    adam_total = lax.psum(adam_part, "fsdp")
+    live = valid_slot.astype(jnp.float32)
+    adam_out = (jnp.take(adam_part, block_index) * live).reshape(owners, load_max)
+    adam_in = lax.all_to_all(adam_out, "fsdp", split_axis=0, concat_axis=0, tiled=True)
+    adam_total = jnp.sum(adam_in, axis=0)
     outgoing = jnp.take(summed, block_index, axis=0) * valid_slot[:, None, None].astype(jnp.float32)
     outgoing = outgoing.reshape(owners, load_max, shard_rows, block_size)
     incoming = lax.all_to_all(outgoing, "fsdp", split_axis=0, concat_axis=2, tiled=True)[0]
@@ -68,17 +75,14 @@
         incoming, left_stat[0, 0], right_stat[0, 0], left_root[0, 0], right_root[0, 0], out_mask
     )
     prec_owner = jnp.sum(precond * precond, axis=(1, 2))
-    spread_sq = jnp.broadcast_to(prec_owner[None, :, None], (1, load_max, owners))
-    back_prec, back_sq = (
-        lax.all_to_all(precond[None], "fsdp", split_axis=2, concat_axis=0, tiled=True),
-        lax.all_to_all(spread_sq, "fsdp", split_axis=2, concat_axis=0, tiled=True),
+    graft = LEARN_RATE * jnp.sqrt(adam_total / (prec_owner + NORM_EPS))
+    back_prec = lax.all_to_all(
+        (precond * graft[:, None, None])[None], "fsdp", split_axis=2, concat_axis=0, tiled=True
     )
     home_prec = jnp.take(
         back_prec.reshape(owners * load_max, shard_rows, block_size), flat_slot, axis=0
     )
-    prec_total = jnp.take(back_sq.reshape(owners * load_max), flat_slot)
-    graft = jnp.sqrt(adam_total / (prec_total + NORM_EPS))
-    new_weight = weights - LEARN_RATE * home_prec * graft[:, None, None]
+    new_weight = weights - home_prec
     return (new_weight, new_moment, left_new[None, None], right_new[None, None])
 
 

time: 340 us -> 169 us (0.50)
  blocking collectives: 153 us -> 0 us
  between operations: 15 us -> 0.96 us
  waiting for transfers between devices: 112 us -> 99.2 us
  starting transfers between devices: 22.4 us -> 30.8 us
    psum x1 -> x0, blocking collectives: 153 us -> none  [on_device(): adam_total = lax.psum(adam_part, 'fsdp')]
    unnamed x2 -> x0, waiting for transfers between devices: 68.2 us -> none
    all_to_all x2 -> x3, waiting for transfers between devices: 5.04 us -> 60.6 us  [the longest x1 31.3 us: on_device(): lax.all_to_all((precond * graft[:, None, None])[None], 'fsdp', split_axis...]
    all_to_all x2 -> x3, starting transfers between devices: 11.7 us -> 26 us  [the longest x1 14.6 us: on_device(): lax.all_to_all(adam_out, 'fsdp', split_axis=0, concat_axis=0, tiled=True)]
    all_to_all x1, starting transfers between devices: 10.7 us -> 4.77 us  [on_device(): lax.all_to_all(outgoing, 'fsdp', split_axis=0, concat_axis=2, tiled=True)[0]]
  transfers between devices with their start and end apart: 4 -> 4, of which waited for: 3 -> 4; matrix products, arithmetic and copies ran while one was open for 5% -> 8% of each run, Pallas kernels for 0% -> 0%
where the time goes in v1:
time: 169 us; the launch traced here: 168 us
  waiting for transfers between devices  99.2 us (59%)
  starting transfers between devices  30.8 us (18%)
  local copies, waits for them, and re-layouts  16.4 us (10%)
  matrix products  10.7 us (6%)
  other arithmetic  10.3 us (6%)
    all_to_all x1, waiting for transfers between devices, on_device(): lax.all_to_all(outgoing, 'fsdp', split_axis=0, concat_axis=2, tiled=True)[0]  38.7 us
    all_to_all x1, waiting for transfers between devices, on_device(): lax.all_to_all((precond * graft[:, None, None])[None], 'fsdp', split_axis...  31.3 us
    all_to_all x1, waiting for transfers between devices, on_device(): lax.all_to_all(grads[0].reshape(tp_size, count_blocks, shard_rows, block_...  22.3 us
    all_to_all x1, starting transfers between devices, on_device(): lax.all_to_all(adam_out, 'fsdp', split_axis=0, concat_axis=0, tiled=True)  14.6 us
    all_to_all x1, waiting for transfers between devices, on_device(): lax.all_to_all(adam_out, 'fsdp', split_axis=0, concat_axis=0, tiled=True)  6.91 us
    all_to_all x1, starting transfers between devices, on_device(): lax.all_to_all((precond * graft[:, None, None])[None], 'fsdp', split_axis...  6.49 us
    all_to_all x1, starting transfers between devices, on_device(): lax.all_to_all(grads[0].reshape(tp_size, count_blocks, shard_rows, block_...  4.99 us
    all_to_all x1, starting transfers between devices, on_device(): lax.all_to_all(outgoing, 'fsdp', split_axis=0, concat_axis=2, tiled=True)[0]  4.77 us
  transfers between devices with their start and end apart: 4, of which 4 were waited for; matrix products, arithmetic and copies ran while one was open for 8% of the time, Pallas kernels for 0%

profile of v1, /device:TPU:1, one launch (start us, length us, event | category | flops | bytes accessed | tf_op | source)
XLA Modules:
  0.0 168.4 jit_solution(5960964115853512726)
XLA Ops:
  0.6 0.0 copy-start
  0.7 5.0 %all-to-all-start = ((f32[4,128,4,256]{3,2,1,0:T(4,128)}), f32[4,128,4,256]{3,2,1,0:T(4,128)S(1)}, u32[]{:S(2)}, u32[]{:S(2)}) async-start(f32[4,128,4,256]{3,2,1,0:T(4,128)} %bitcast.46), calls=%async_computation | async-start | bytes 4194304 | tf_op jit(solution)/shard_map/all_to_all | solution.py:53
  5.7 0.1 fusion.7
  5.7 0.2 reduce_window_sum.11
  5.9 0.2 select_reduce_fusion.1
  6.1 0.5 compare_and_fusion.2
  6.6 0.1 fusion.6
  6.7 0.1 reduce_or.12
  6.9 0.1 select_reduce_fusion
  7.0 0.1 reduce_sum.62
  7.1 0.1 reduce_sum.65
  7.3 0.1 reshape.223
  7.5 0.1 broadcast_compare_fusion
  7.6 0.1 iota_compare_fusion.1
  7.7 22.3 %all-to-all-done = f32[4,128,4,256]{3,2,1,0:T(4,128)S(1)} async-done(((f32[4,128,4,256]{3,2,1,0:T(4,128)}), f32[4,128,4,256]{3,2,1,0:T(4,128)S(1)}, u32[]{:S(2)}, u32[]{:S(2)}) %all-to-all-start) | async-done | bytes 2097184 | tf_op jit(solution)/shard_map/all_to_all | solution.py:53
  30.0 0.6 reduce_sum.63
  30.6 3.7 %multiply_reduce_fusion.1 = (f32[128]{0:T(128)S(1)}, f32[128,4,256]{2,1,0:T(4,128)}, f32[128,4,256]{2,1,0:T(4,128)S(1)}) fusion(f32[128,4,256]{2,1,0:T(4,128)} %param.11, f32[128,4,256]{2,1,0:T(4,128)S(1)} %reduce_sum.63, pred[128,256]{1,0:T(8,128)(4,1)S(1)} %iota_compare_fusion.1, pred[128,4]{1,0:T(8,128)(4,1)S(1)} %broadcast_compare_fusion), kind=kLoop, calls=%fused_computation.18 | loop fusion | flops 1310592 | bytes 2130944 | tf_op jit(solution)/shard_map/reduce_sum | solution.py:62
  34.3 2.5 %gather_fusion.1 = f32[384,4,256]{2,1,0:T(4,128)S(1)} fusion(f32[128,4,256]{2,1,0:T(4,128)S(1)} %get-tuple-element.10, s32[1024]{0:T(1024)S(1)} %pad_clamp_fusion.1), kind=kCustom, calls=%fused_computation.1 | custom fusion | bytes 3147264 | tf_op jit(solution)/shard_map/jit(_take)/gather | solution.py:68
  36.8 2.7 %gather_fusion.2 = f32[384]{0:T(512)S(1)} fusion(f32[128]{0:T(128)S(1)} %get-tuple-element.8, s32[1024]{0:T(1024)S(1)} %pad_clamp_fusion.1), kind=kCustom, calls=%fused_computation.2 | custom fusion | bytes 4608 | tf_op jit(solution)/shard_map/jit(_take)/gather | solution.py:65
  39.5 0.1 gather.24
  39.6 0.6 select_select_fusion
  40.2 14.6 %all-to-all-start.2 = ((f32[64,1,6]{2,1,0:T(1,128)}), f32[64,1,6]{2,1,0:T(1,128)S(1)}, u32[]{:S(2)}, u32[]{:S(2)}) async-start(f32[64,1,6]{2,1,0:T(1,128)} %bitcast.8), calls=%async_computation.2 | async-start | bytes 65536 | tf_op jit(solution)/shard_map/all_to_all | solution.py:66
  54.8 2.3 %select_multiply_fusion = f32[64,6,4,256]{3,2,1,0:T(4,128)} fusion(f32[64,6,4,256]{3,2,1,0:T(4,128)S(1)} %bitcast.44, f32[64,6]{1,0:T(8,128)S(1)} %reshape.223, pred[64,6]{1,0:T(8,128)(4,1)S(1)} %compare_and_fusion), kind=kLoop, calls=%fused_computation.10 | loop fusion | flops 786432 | bytes 3147648 | tf_op jit(solution)/shard_map/mul | solution.py:68
  57.1 6.9 %all-to-all-done.2 = f32[64,1,6]{2,1,0:T(1,128)S(1)} async-done(((f32[64,1,6]{2,1,0:T(1,128)}), f32[64,1,6]{2,1,0:T(1,128)S(1)}, u32[]{:S(2)}, u32[]{:S(2)}) %all-to-all-start.2) | async-done | bytes 1568 | tf_op jit(solution)/shard_map/all_to_all | solution.py:66
  64.0 4.8 %all-to-all-start.1 = ((f32[64,6,4,256]{3,2,1,0:T(4,128)}), f32[64,6,4,256]{3,2,1,0:T(4,128)S(1)}, u32[]{:S(2)}, u32[]{:S(2)}) async-start(f32[64,6,4,256]{3,2,1,0:T(4,128)} %select_multiply_fusion), calls=%async_computation.1 | async-start | bytes 3145728 | tf_op jit(solution)/shard_map/all_to_all | solution.py:70
  68.8 0.1 copy.56
  68.9 0.1 compare_and_fusion.1
  69.0 0.6 gather_fusion
  69.6 0.1 broadcast_select_fusion
  69.6 0.2 multiply_reduce_fusion.3
  69.8 0.1 iota_compare_fusion.3
  69.9 0.1 reduce_sum.67
  70.0 38.7 %all-to-all-done.1 = f32[64,6,4,256]{3,2,1,0:T(4,128)S(1)} async-done(((f32[64,6,4,256]{3,2,1,0:T(4,128)}), f32[64,6,4,256]{3,2,1,0:T(4,128)S(1)}, u32[]{:S(2)}, u32[]{:S(2)}) %all-to-all-start.1) | async-done | bytes 1572896 | tf_op jit(solution)/shard_map/all_to_all | solution.py:70
  108.6 1.4 copy.57
  110.0 1.9 %squeeze.11 = f32[6,256,256]{2,1,0:T(8,128)S(1)} reshape(f32[1,6,64,4,256]{4,3,2,1,0:T(4,128)} %copy.57) | data formatting | bytes 3145728 | tf_op jit(solution)/shard_map/squeeze | solution.py:70
  112.0 1.0 fusion.3
  112.9 1.4 multiply_reduce_fusion
  114.4 0.2 multiply_bitcast_fusion
  114.6 2.8 %copy.61 = f32[1,6,256,256]{3,0,1,2:T(1,128)} copy(f32[1,6,256,256]{3,2,1,0:T(8,128)S(1)} %multiply_bitcast_fusion) | data formatting | bytes 3145728 | tf_op jit(solution)/shard_map/broadcast_in_dim | solution.py:80
  117.4 6.5 %all-to-all-start.3 = ((f32[1,6,256,256]{3,0,1,2:T(1,128)}), f32[1,6,256,256]{3,0,1,2:T(1,128)}, u32[]{:S(2)}, u32[]{:S(2)}) async-start(f32[1,6,256,256]{3,0,1,2:T(1,128)} %copy.61), calls=%async_computation.3 | async-start | bytes 3145728 | tf_op jit(solution)/shard_map/all_to_all | solution.py:79
  123.9 0.0 copy-start.1
  123.9 4.5 %fusion.1 = f32[1,1,6,256,256]{4,3,2,1,0:T(8,128)} fusion(f32[1,1,6,256,256]{4,3,2,1,0:T(8,128)} %param.12, f32[6,256,256]{2,1,0:T(8,128)S(1)} %squeeze.11), kind=kOutput, calls=%fused_computation.7 | convolution fusion | flops 1209139200 | bytes 4718592 | tf_op jit(solution)/shard_map/sij,skj->sik/dot_general | solution.py:34
  128.4 3.9 %fusion = f32[1,1,6,256,256]{4,3,2,1,0:T(8,128)} fusion(f32[1,1,6,256,256]{4,3,2,1,0:T(8,128)S(1)} %copy-done.1, f32[6,256,256]{2,1,0:T(8,128)S(1)} %squeeze.11), kind=kOutput, calls=%fused_computation.5 | convolution fusion | flops 1209139200 | bytes 4718592 | tf_op jit(solution)/shard_map/sji,sjk->sik/dot_general | solution.py:35
  132.3 31.3 %all-to-all-done.3 = f32[1,6,256,256]{3,0,1,2:T(1,128)} async-done(((f32[1,6,256,256]{3,0,1,2:T(1,128)}), f32[1,6,256,256]{3,0,1,2:T(1,128)}, u32[]{:S(2)}, u32[]{:S(2)}) %all-to-all-start.3) | async-done | bytes 1572896 | tf_op jit(solution)/shard_map/all_to_all | solution.py:79
  163.6 2.5 %copy.62 = f32[1,6,256,256]{3,0,2,1:T(1,128)S(1)} copy(f32[1,6,256,256]{3,0,1,2:T(1,128)} %all-to-all-done.3) | data formatting | bytes 3145728 | tf_op jit(solution)/shard_map/all_to_all | solution.py:79
  166.1 0.4 copy.63
  166.5 0.9 gather_fusion.3
  167.4 1.0 select_subtract_fusion
  (26 shorter events, 0.1 us)
Async XLA Ops:
  0.6 112.3 %copy-start = (bf16[1,1,6,256,256]{4,3,2,1,0:T(8,128)(2,1)S(1)}, bf16[1,1,6,256,256]{4,3,2,1,0:T(8,128)(2,1)}, u32[]{:S(2)}) copy-start(bf16[1,1,6,256,256]{4,3,2,1,0:T(8,128)(2,1)} %param.15) | copy-start | bytes 2359300
  0.6 5.0 %copy-start.4 = (s32[128]{0:T(128)S(1)}, s32[128]{0:T(128)}, u32[]{:S(2)}) copy-start(s32[128]{0:T(128)} %param.16) | copy-start | bytes 1540
  0.7 6.8 %copy-start.5 = (s32[128,2]{0,1:T(2,128)S(1)}, s32[128,2]{0,1:T(2,128)}, u32[]{:S(2)}) copy-start(s32[128,2]{0,1:T(2,128)} %param.17) | copy-start | bytes 3076
  0.7 29.4 %all-to-all-start = ((f32[4,128,4,256]{3,2,1,0:T(4,128)}), f32[4,128,4,256]{3,2,1,0:T(4,128)S(1)}, u32[]{:S(2)}, u32[]{:S(2)}) async-start(f32[4,128,4,256]{3,2,1,0:T(4,128)} %bitcast.46), calls=%async_computation | async-start | bytes 4194304 | tf_op jit(solution)/shard_map/all_to_all | solution.py:53
  6.6 0.8 copy-start.7
  40.2 23.8 %all-to-all-start.2 = ((f32[64,1,6]{2,1,0:T(1,128)}), f32[64,1,6]{2,1,0:T(1,128)S(1)}, u32[]{:S(2)}, u32[]{:S(2)}) async-start(f32[64,1,6]{2,1,0:T(1,128)} %bitcast.8), calls=%async_computation.2 | async-start | bytes 65536 | tf_op jit(solution)/shard_map/all_to_all | solution.py:66
  64.0 44.6 %all-to-all-start.1 = ((f32[64,6,4,256]{3,2,1,0:T(4,128)}), f32[64,6,4,256]{3,2,1,0:T(4,128)S(1)}, u32[]{:S(2)}, u32[]{:S(2)}) async-start(f32[64,6,4,256]{3,2,1,0:T(4,128)} %select_multiply_fusion), calls=%async_computation.1 | async-start | bytes 3145728 | tf_op jit(solution)/shard_map/all_to_all | solution.py:70
  110.0 1.9 %copy-start.2 = (bf16[1,1,6,256,256]{4,3,2,1,0:T(8,128)(2,1)S(1)}, bf16[1,1,6,256,256]{4,3,2,1,0:T(8,128)(2,1)}, u32[]{:S(2)}) copy-start(bf16[1,1,6,256,256]{4,3,2,1,0:T(8,128)(2,1)} %param.14) | copy-start | bytes 2359300
  117.4 6.5 %copy-start.8 = (s32[128]{0:T(128)S(1)}, s32[128]{0:T(128)}, u32[]{:S(2)}) copy-start(s32[128]{0:T(128)} %copy-done.7) | copy-start | bytes 1540
  117.4 46.2 %all-to-all-start.3 = ((f32[1,6,256,256]{3,0,1,2:T(1,128)}), f32[1,6,256,256]{3,0,1,2:T(1,128)}, u32[]{:S(2)}, u32[]{:S(2)}) async-start(f32[1,6,256,256]{3,0,1,2:T(1,128)} %copy.61), calls=%async_computation.3 | async-start | bytes 3145728 | tf_op jit(solution)/shard_map/all_to_all | solution.py:79
  123.9 4.5 %copy-start.1 = (f32[1,1,6,256,256]{4,3,2,1,0:T(8,128)S(1)}, f32[1,1,6,256,256]{4,3,2,1,0:T(8,128)}, u32[]{:S(2)}) copy-start(f32[1,1,6,256,256]{4,3,2,1,0:T(8,128)} %param.13) | copy-start | bytes 4718596
  166.1 1.3 copy-start.3
  166.1 1.3 copy-start.6

commit v2 on v0

v2 whole, which is shorter than its diff:
```python
import functools

import jax
import jax.numpy as jnp
from jax import lax
from jax.experimental import pallas as pl
from jax.experimental.pallas import tpu as pltpu
from jax.sharding import PartitionSpec as P

ADAM_BETA = 0.95
STAT_BETA = 0.99
LEARN_RATE = 0.05
ADAM_EPS = 1e-08
NORM_EPS = 1e-06

NX, NY, NZ, NC = 4, 4, 8, 2
NYC = NY * NC
COLUMN = 128
SLOTS = 6
HALF = 128
MESH = pl.DeviceIdType.MESH
Z_ORDER = (4, 3, 5, 2, 6, 1, 7, 0)
F32 = jnp.float32
BF16 = jnp.bfloat16


def split(value):
    high = value.astype(BF16)
    low = (value - high.astype(F32)).astype(BF16)
    return high, low


def dot(a, b, dims=((1,), (0,))):
    return lax.dot_general(a, b, (dims, ((), ())), preferred_element_type=F32)


def step_kernel(
    cap,
    zpack, ypack, bpack, home, own_info,
    mask, own_hot, grads, moments, weights, left, right, left_root, right_root,
    new_w, new_m, new_left, new_right,
    *scratch,
):
    scratch = list(scratch)
    zr = [[scratch.pop(0) for _ in range(NZ)] for _ in range(2)]
    ybr = [scratch.pop(0) for _ in range(NZ)]
    summed = [scratch.pop(0) for _ in range(2)]
    (own_part, parts, mom, mom_out, arow, zsb, ysb, yr, gfull, lroot, rroot, lstat, rstat,
     ybs, zbs, zbr, wbuf,
     rs_send, rs_recv, z_send, z_recv, y_send, y_recv, yb_send, yb_recv, zb_send, zb_recv,
     loc_sem, in_sem, out_sem) = scratch

    me = lax.axis_index("fsdp")
    my_x = lax.axis_index("tp")
    my_c = lax.rem(me, NC)
    my_z = lax.rem(lax.div(me, NC), NZ)
    my_y = lax.div(me, NC * NZ)
    my_yc = my_y * NC + my_c

    def index_of(y, z, c):
        return (y * NZ + z) * NC + c

    def z_peer(d):
        return {"fsdp": index_of(my_y, lax.rem(my_z + d, NZ), my_c)}

    def yc_at(e):
        return lax.rem(my_y + e // NC, NY), lax.rem(my_c + e % NC, NC)

    def yc_peer(e):
        y, c = yc_at(e)
        return {"fsdp": index_of(y, my_z, c)}

    def yc_index(e):
        y, c = yc_at(e)
        return y * NC + c

    def x_peer(d):
        return {"tp": lax.rem(my_x + d, NX)}

    barrier = pltpu.get_barrier_semaphore()
    peers = [x_peer(d) for d in range(1, NX)] + [z_peer(d) for d in range(1, NZ)] + [yc_peer(e) for e in range(1, NYC)]
    for peer in peers:
        pl.semaphore_signal(barrier, inc=1, device_id=peer, device_id_type=MESH)
    own_copies = [
        pltpu.make_async_copy(grads.at[pl.ds(my_x * COLUMN, COLUMN), h], own_part.at[h], loc_sem.at[h]) for h in range(2)
    ]
    mom_copies = [pltpu.make_async_copy(moments.at[:, h], mom.at[h], loc_sem.at[2 + h]) for h in range(2)]
    for copy in own_copies + mom_copies:
        copy.start()
    pl.semaphore_wait(barrier, len(peers))

    rs = []
    for h in range(2):
        row = []
        for d in (2, 1, 3):
            there = lax.rem(my_x + d, NX)
            copy = pltpu.make_async_remote_copy(
                src_ref=grads.at[pl.ds(there * COLUMN, COLUMN), h], dst_ref=parts.at[h, d - 1],
                send_sem=rs_send.at[h, d - 1], recv_sem=rs_recv.at[h, d - 1],
                device_id=x_peer(d), device_id_type=MESH,
            )
            copy.start()
            row.append(copy)
        rs.append(row)
    big_in = [
        pltpu.make_async_copy(left_root, lroot, in_sem.at[0]),
        pltpu.make_async_copy(right_root, rroot, in_sem.at[1]),
        pltpu.make_async_copy(left, lstat, in_sem.at[2]),
        pltpu.make_async_copy(right, rstat, in_sem.at[3]),
        pltpu.make_async_copy(weights, wbuf, in_sem.at[4]),
    ]
    for copy in big_in:
        copy.start()

    chunk = 8
    out_copies = []
    z_copies = [[None] * NZ for _ in range(2)]
    for h in range(2):
        own_copies[h].wait()
        mom_copies[h].wait()
        for copy in rs[h]:
            copy.wait_recv()

        @pl.loop(0, COLUMN // chunk)
        def _(i):
            rows = pl.ds(i * chunk, chunk)
            total = (own_part[h, rows] + parts[h, 0, rows]) + (parts[h, 1, rows] + parts[h, 2, rows])
            total = total * mask[h, rows]
            moment = ADAM_BETA * mom[h, rows] + (1.0 - ADAM_BETA) * total * total
            summed[h][rows] = total
            mom_out[h, rows] = moment
            direction = total / (jnp.sqrt(moment) + ADAM_EPS)
            arow[rows, :] = jnp.sum(direction * direction, axis=1)

        out_copy = pltpu.make_async_copy(mom_out.at[h], new_m.at[:, h], out_sem.at[h])
        out_copy.start()
        out_copies.append(out_copy)
        adam = lax.dot_general(
            jnp.ones((8, COLUMN), F32), arow[...], (((1,), (1,)), ((), ())),
            precision=lax.Precision.HIGHEST, preferred_element_type=F32,
        )[0:4]
        for d in Z_ORDER:
            there = lax.rem(my_z + d, NZ)
            target = zr[h][0] if d == 0 else zsb.at[h, d - 1]
            base = there * cap

            @pl.loop(0, cap, step=8)
            def _(k0):
                for u in range(8):
                    target[k0 + u] = summed[h][zpack[base + k0 + u]]

            target[cap] = adam
            if d:
                copy = pltpu.make_async_remote_copy(
                    src_ref=zsb.at[h, d - 1], dst_ref=zr[h][d],
                    send_sem=z_send.at[h, d - 1], recv_sem=z_recv.at[h, d - 1],
                    device_id=z_peer(d), device_id_type=MESH,
                )
                copy.start()
                z_copies[h][d] = copy

    for h in range(2):
        for d in (0,) + Z_ORDER[:-1]:
            if d:
                z_copies[h][d].wait_recv()
            source_z = lax.rem(my_z + (NZ - d), NZ)
            for e in range(NYC):
                base = yc_index(e) * SLOTS
                target = ysb.at[h, e - 1, d] if e else yr.at[h, my_yc, source_z]
                for j in range(SLOTS):
                    target[j] = zr[h][d][ypack[base + j]]
                target[SLOTS] = zr[h][d][cap]
                if e:
                    pltpu.make_async_remote_copy(
                        src_ref=ysb.at[h, e - 1, d], dst_ref=yr.at[h, my_yc, source_z],
                        send_sem=y_send.at[h], recv_sem=y_recv.at[h],
                        device_id=yc_peer(e), device_id_type=MESH,
                    ).start()

    def y_all(h):
        return pltpu.make_async_remote_copy(
            src_ref=ysb.at[h], dst_ref=yr.at[h, pl.ds(0, NYC - 1)],
            send_sem=y_send.at[h], recv_sem=y_recv.at[h],
            device_id=yc_peer(1), device_id_type=MESH,
        )

    adam_total = jnp.zeros((4, COLUMN), F32)
    for h in range(2):
        y_all(h).wait_recv()

        def build(t, total, h=h):
            y, zs = lax.div(t, NZ), lax.rem(t, NZ)
            for j in range(SLOTS):
                tile = jnp.concatenate([yr[h, y * NC, zs, j], yr[h, y * NC + 1, zs, j]], axis=0)
                tile = jnp.where(own_info[j] > 0, tile, 0.0)
                gfull[j, pl.ds(pl.multiple_of(t * 8, 8), 8), h * HALF:(h + 1) * HALF] = tile
            return total + (yr[h, y * NC, zs, SLOTS] + yr[h, y * NC + 1, zs, SLOTS])

        adam_total = lax.fori_loop(0, NY * NZ, build, adam_total)

    big_in[0].wait()
    big_in[1].wait()
    row_ids = lax.broadcasted_iota(jnp.int32, (2 * HALF, 2 * HALF), 0)
    col_ids = lax.broadcasted_iota(jnp.int32, (2 * HALF, 2 * HALF), 1)
    adam_row = adam_total[0:1]

    @pl.loop(0, SLOTS)
    def _(j):
        high, low = split(gfull[j])
        inner = dot(lroot[j], high) + dot(lroot[j], low)
        in_high, in_low = split(inner)
        prec = dot(in_high, rroot[j]) + dot(in_low, rroot[j])
        live = (row_ids < own_info[8 + j] * HALF) & (col_ids < own_info[16 + j] * HALF)
        prec = jnp.where(live, prec, 0.0)
        prec_sq = jnp.sum(prec * prec)
        adam_sq = jnp.sum(own_hot[pl.ds(j, 1), :] * adam_row)
        graft = LEARN_RATE * jnp.sqrt(jnp.full((1, HALF), adam_sq) / (jnp.full((1, HALF), prec_sq) + NORM_EPS))
        left_cols = (prec[:, :HALF] * graft).reshape(NY * NZ, 8, HALF)
        right_cols = (prec[:, HALF:] * graft).reshape(NY * NZ, 8, HALF)
        for core in range(NC):
            rows = slice(core * 4, core * 4 + 4)
            piece = jnp.concatenate([left_cols[:, rows], right_cols[:, rows]], axis=1)
            for y in range(NY):
                ybs[y * NC + core, :, j] = piece[y * NZ:(y + 1) * NZ]

    for d in Z_ORDER:
        dest_z = lax.rem(my_z + d, NZ)
        for e in range(1, NYC):
            pltpu.make_async_remote_copy(
                src_ref=ybs.at[yc_index(e), dest_z], dst_ref=ybr[d].at[pl.ds(my_yc * SLOTS, SLOTS)],
                send_sem=yb_send, recv_sem=yb_recv.at[d],
                device_id=yc_peer(e), device_id_type=MESH,
            ).start()

    zb_copies = []
    for d in Z_ORDER:
        dest_z = lax.rem(my_z + d, NZ)
        ybr[d][pl.ds(my_yc * SLOTS, SLOTS)] = ybs[my_yc, dest_z]
        pltpu.make_async_remote_copy(
            src_ref=ybr[d].at[pl.ds(0, (NYC - 1) * SLOTS)], dst_ref=ybr[d].at[pl.ds(0, (NYC - 1) * SLOTS)],
            send_sem=yb_send, recv_sem=yb_recv.at[d],
            device_id=yc_peer(1), device_id_type=MESH,
        ).wait_recv()
        target = zbr.at[pl.ds(my_z * cap, cap)] if d == 0 else zbs.at[d - 1]

        @pl.loop(0, cap, step=8)
        def _(k0):
            for u in range(8):
                target[k0 + u] = ybr[d][bpack[k0 + u]]

        if d:
            copy = pltpu.make_async_remote_copy(
                src_ref=zbs.at[d - 1], dst_ref=zbr.at[pl.ds(my_z * cap, cap)],
                send_sem=zb_send.at[d - 1], recv_sem=zb_recv.at[d - 1],
                device_id=z_peer(d), device_id_type=MESH,
            )
            copy.start()
            zb_copies.append(copy)

    big_in[2].wait()
    big_in[3].wait()

    @pl.loop(0, SLOTS)
    def _(j):
        high, low = split(gfull[j])
        rows = ((1,), (1,))
        outer = dot(high, high, rows) + (dot(high, low, rows) + dot(low, high, rows))
        lstat[j] = STAT_BETA * lstat[j] + (1.0 - STAT_BETA) * outer
        cols = ((0,), (0,))
        outer = dot(high, high, cols) + (dot(high, low, cols) + dot(low, high, cols))
        rstat[j] = STAT_BETA * rstat[j] + (1.0 - STAT_BETA) * outer

    for i, (source, out) in enumerate(((lstat, new_left), (rstat, new_right))):
        out_copy = pltpu.make_async_copy(source, out, out_sem.at[2 + i])
        out_copy.start()
        out_copies.append(out_copy)

    big_in[4].wait()
    for copy in zb_copies:
        copy.wait_recv()

    @pl.loop(0, COLUMN, step=8)
    def _(b0):
        for u in range(8):
            new_w[b0 + u] = wbuf[b0 + u] - zbr[home[b0 + u]]

    for h in range(2):
        for copy in rs[h]:
            copy.wait_send()
        for d in range(1, NZ):
            z_copies[h][d].wait_send()
        y_all(h).wait_send()
    pltpu.make_async_remote_copy(
        src_ref=ybs.at[pl.ds(0, NYC - 1)], dst_ref=ybs.at[pl.ds(0, NYC - 1)],
        send_sem=yb_send, recv_sem=yb_recv.at[0],
        device_id=yc_peer(1), device_id_type=MESH,
    ).wait_send()
    for copy in zb_copies:
        copy.wait_send()
    for copy in out_copies:
        copy.wait()


def tables(owner, extent, cap):
    me = lax.axis_index("fsdp").astype(jnp.int32)
    my_z = (me // NC) % NZ
    ids = jnp.arange(COLUMN, dtype=jnp.int32)
    plane = (owner // NC) % NZ
    yc = (owner // (NC * NZ)) * NC + owner % NC
    before = ids[None, :] < ids[:, None]
    rank_owner = jnp.sum((before & (owner[None, :] == owner[:, None])).astype(jnp.int32), axis=1)
    rank_plane = jnp.sum((before & (plane[None, :] == plane[:, None])).astype(jnp.int32), axis=1)
    home = plane * cap + rank_plane
    slot = yc * SLOTS + rank_owner

    def invert(keys, size, values):
        hits = keys[None, :] == jnp.arange(size, dtype=jnp.int32)[:, None]
        return jnp.sum(jnp.where(hits, values[None, :], 0), axis=1)

    here = plane == my_z
    zpack = invert(home, NZ * cap, ids)
    ypack = invert(jnp.where(here, slot, -1), NYC * SLOTS, rank_plane)
    bpack = invert(jnp.where(here, rank_plane, -1), cap, slot)
    mine = jnp.where(owner == me, rank_owner, -1)
    own_hot = (mine[None, :] == jnp.arange(8, dtype=jnp.int32)[:, None])
    own_info = jnp.concatenate([
        jnp.sum(own_hot.astype(jnp.int32), axis=1),
        jnp.sum(jnp.where(own_hot, extent[None, :, 0], 0), axis=1),
        jnp.sum(jnp.where(own_hot, extent[None, :, 1], 0), axis=1),
    ])
    row_live = me * 4 < extent[:, 0] * HALF
    col_live = jnp.arange(2, dtype=jnp.int32)[:, None] < extent[None, :, 1]
    live = (row_live[None, :] & col_live).astype(F32)
    mask = jnp.broadcast_to(live[:, :, None, None], (2, COLUMN, 1, HALF))
    return zpack, ypack, bpack, home, own_info, mask, own_hot.astype(F32)


def run_step(cap, grads, weights, moments, left_stat, right_stat, left_root, right_root, owner, extent):
    piece = (4, HALF)
    any_spec = pl.BlockSpec(memory_space=pl.ANY)
    smem = pl.BlockSpec(memory_space=pltpu.SMEM)
    vmem = pl.BlockSpec(memory_space=pltpu.VMEM)
    size = 2 * HALF
    dma = pltpu.SemaphoreType.DMA
    scratch = (
        [pltpu.VMEM((cap + 1,) + piece, F32) for _ in range(2 * NZ)]
        + [pltpu.VMEM((NYC * SLOTS, 8, HALF), F32) for _ in range(NZ)]
        + [pltpu.VMEM((COLUMN,) + piece, F32) for _ in range(2)]
        + [
            pltpu.VMEM((2, COLUMN) + piece, F32),
            pltpu.VMEM((2, NX - 1, COLUMN) + piece, F32),
            pltpu.VMEM((2, COLUMN) + piece, F32),
            pltpu.VMEM((2, COLUMN) + piece, F32),
            pltpu.VMEM((COLUMN, HALF), F32),
            pltpu.VMEM((2, NZ - 1, cap + 1) + piece, F32),
            pltpu.VMEM((2, NYC - 1, NZ, SLOTS + 1) + piece, F32),
            pltpu.VMEM((2, NYC, NZ, SLOTS + 1) + piece, F32),
            pltpu.VMEM((SLOTS, size, size), F32),
            pltpu.VMEM((SLOTS, size, size), BF16),
            pltpu.VMEM((SLOTS, size, size), BF16),
            pltpu.VMEM((SLOTS, size, size), F32),
            pltpu.VMEM((SLOTS, size, size), F32),
            pltpu.VMEM((NYC, NZ, SLOTS, 8, HALF), F32),
            pltpu.VMEM((NZ - 1, cap, 8, HALF), F32),
            pltpu.VMEM((NZ * cap, 8, HALF), F32),
            pltpu.VMEM((COLUMN, 8, HALF), F32),
            dma((2, NX - 1)), dma((2, NX - 1)),
            dma((2, NZ - 1)), dma((2, NZ - 1)),
            dma((2,)), dma((2,)),
            dma, dma((NZ,)),
            dma((NZ - 1,)), dma((NZ - 1,)),
            dma((4,)), dma((5,)), dma((4,)),
        ]
    )
    halves = lambda a: a.reshape(-1, 4, 2, HALF).transpose(0, 2, 1, 3)
    zpack, ypack, bpack, home, own_info, mask, own_hot = tables(owner, extent, cap)
    new_w, new_m, new_left, new_right = pl.pallas_call(
        functools.partial(step_kernel, cap),
        out_shape=(
            jax.ShapeDtypeStruct((COLUMN, 8, HALF), F32),
            jax.ShapeDtypeStruct((COLUMN, 2) + piece, F32),
            jax.ShapeDtypeStruct((SLOTS, size, size), F32),
            jax.ShapeDtypeStruct((SLOTS, size, size), F32),
        ),
        in_specs=[smem] * 5 + [vmem] * 2 + [any_spec] * 7,
        out_specs=(vmem, any_spec, any_spec, any_spec),
        scratch_shapes=scratch,
        compiler_params=pltpu.CompilerParams(
            collective_id=0, has_side_effects=True, vmem_limit_bytes=48 * 1024 * 1024
        ),
        name="step",
    )(
        zpack, ypack, bpack, home, own_info, mask, own_hot,
        halves(grads[0]), halves(moments), halves(weights).reshape(COLUMN, 8, HALF),
        left_stat[0, 0], right_stat[0, 0], left_root[0, 0], right_root[0, 0],
    )
    whole = lambda a: a.reshape(COLUMN, 2, 4, HALF).transpose(0, 2, 1, 3).reshape(COLUMN, 4, size)
    return whole(new_w), whole(new_m), new_left[None, None], new_right[None, None]


def on_device(*args):
    return run_step(NYC * SLOTS, *args)


def solution(mesh):
    in_specs = (
        P("tp", None, "fsdp", None),
        P("tp", "fsdp", None),
        P("tp", "fsdp", None),
        P("tp", "fsdp", None, None, None),
        P("tp", "fsdp", None, None, None),
        P("tp", "fsdp", None, None, None),
        P("tp", "fsdp", None, None, None),
        P("tp"),
        P("tp", None),
    )
    out_specs = (
        P("tp", "fsdp", None),
        P("tp", "fsdp", None),
        P("tp", "fsdp", None, None, None),
        P("tp", "fsdp", None, None, None),
    )
    return jax.shard_map(
        on_device, mesh=mesh, in_specs=in_specs, out_specs=out_specs, check_vma=False
    )
```

time: 340 us -> 129 us (0.38)
  blocking collectives: 153 us -> 0 us
  Pallas kernels: 0 us -> 115 us
  waiting for transfers between devices: 112 us -> 0 us
  starting transfers between devices: 22.4 us -> 0 us
  between operations: 15 us -> 0.72 us
  matrix products: 11.6 us -> 0 us
  local copies, waits for them, and re-layouts: 17.3 us -> 10.1 us
  other arithmetic: 8.41 us -> 2.94 us
    psum x1 -> x0, blocking collectives: 153 us -> none  [on_device(): adam_total = lax.psum(adam_part, 'fsdp')]
    pallas_call x0 -> x1, Pallas kernels: none -> 115 us  [run_step(): pl.pallas_call(functools.partial(step_kernel, cap), out_shape=(jax.ShapeD...]
    unnamed x2 -> x0, waiting for transfers between devices: 68.2 us -> none
    all_to_all x3 -> x0, waiting for transfers between devices: 43.7 us -> none  [the longest x1 38.7 us: on_device(): lax.all_to_all(outgoing, 'fsdp', split_axis=0, concat_axis=2, tiled=True)[0]]
    all_to_all x3 -> x0, starting transfers between devices: 22.3 us -> none  [the longest x1 10.7 us: on_device(): lax.all_to_all(outgoing, 'fsdp', split_axis=0, concat_axis=2, tiled=True)[0]]
    dot_general x4 -> x0, matrix products: 11.6 us -> none  [the longest x1 4.46 us: refresh(): jnp.einsum('sij,skj->sik', slot_grad, slot_grad, precision=PRECISE)]
    unnamed x18 -> x14, local copies, waits for them, and re-layouts: 0.74 us -> 9.05 us
    gather x4 -> x0, local copies, waits for them, and re-layouts: 5.16 us -> none  [the longest x1 2.46 us: on_device(): jnp.take(summed, block_index, axis=0)]
  transfers between devices with their start and end apart: 4 -> 0, of which waited for: 3 -> 0; matrix products, arithmetic and copies ran while one was open for 5% -> 0% of each run, Pallas kernels for 0% -> 0%
where the time goes in v2:
time: 129 us
  Pallas kernels  115 us (89%)
  local copies, waits for them, and re-layouts  10.1 us (8%)
  other arithmetic  2.94 us (2%)
    pallas_call x1, Pallas kernels, run_step(): pl.pallas_call(functools.partial(step_kernel, cap), out_shape=(jax.ShapeD...  115 us
    unnamed x14, local copies, waits for them, and re-layouts  9.05 us

profile of v2, /device:TPU:1, one launch (start us, length us, event | category | flops | bytes accessed | tf_op | source)
XLA Modules:
  0.0 128.8 jit_solution(14946135594981279067)
XLA Ops:
  0.7 0.7 multiply_compare_fusion
  1.4 0.9 convert_reduce_fusion
  2.3 0.7 compare_select_fusion.4
  2.9 0.2 convert_reduce_fusion.1
  3.1 0.1 select_reduce_fusion.1
  3.2 0.8 slice_bitcast_fusion.1
  4.0 0.1 convert_reduce_fusion.2
  4.2 0.1 pad_add_fusion.own_info
  4.2 0.2 select_reduce_fusion.zpack
  4.4 0.3 broadcast_in_dim.97.mask
  4.7 0.0 copy-start
  4.7 1.1 copy-done
  5.9 0.0 copy-start.1
  5.9 1.1 copy-done.1
  7.0 0.0 copy-start.2
  7.0 1.0 copy-done.2
  8.0 0.0 copy-start.3
  8.0 1.0 copy-done.3
  9.1 115.0 %step.1 = (f32[128,8,128]{2,1,0:T(8,128)S(1)}, f32[128,2,4,128]{3,2,1,0:T(4,128)S(1)}, f32[6,256,256]{2,1,0:T(8,128)S(1)}, f32[6,256,256]{2,1,0:T(8,128)}) custom-call(s32[384]{0:T(512)S(1)} %select_reduce_fusion.zpack, s32[48]{0:T(128)S(1)} %get-tuple-element.24.ypack, s32[48]{0:T(128)S(1)} %get-tuple-element.23.bpack, s32[128]{0:T(128)S(1)} %get-tuple-element.22.home, ...), custom_call_target="tpu_custom_call" | custom-call | tf_op jit(solution)/shard_map/step/pallas_call | solution.py:377
  124.1 0.8 copy.21
  124.9 0.8 copy.22
  125.7 0.0 copy-start.4
  125.7 1.1 copy.23
  126.8 0.8 copy-done.4
  127.7 1.1 copy.24
  (3 shorter events, 0.0 us)
Async XLA Ops:
  4.7 1.1 copy-start
  5.9 1.1 copy-start.1
  7.0 1.0 copy-start.2
  8.0 1.0 copy-start.3
  125.7 2.0 %copy-start.4 = (f32[6,256,256]{2,1,0:T(8,128)S(1)}, f32[6,256,256]{2,1,0:T(8,128)}, u32[]{:S(2)}) copy-start(f32[6,256,256]{2,1,0:T(8,128)} %get-tuple-element.11) | copy-start | bytes 4718596

commit v3 on v2

--- a/solution.py
+++ b/solution.py
@@ -18,6 +18,8 @@
 COLUMN = 128
 SLOTS = 6
 HALF = 128
+FULL = NYC * SLOTS
+CAPS = (32, FULL)
 MESH = pl.DeviceIdType.MESH
 Z_ORDER = (4, 3, 5, 2, 6, 1, 7, 0)
 F32 = jnp.float32
@@ -36,7 +38,7 @@
 
 def step_kernel(
     cap,
-    zpack, ypack, bpack, home, own_info,
+    table,
     mask, own_hot, grads, moments, weights, left, right, left_root, right_root,
     new_w, new_m, new_left, new_right,
     *scratch,
@@ -125,7 +127,7 @@
         def _(i):
             rows = pl.ds(i * chunk, chunk)
             total = (own_part[h, rows] + parts[h, 0, rows]) + (parts[h, 1, rows] + parts[h, 2, rows])
-            total = total * mask[h, rows]
+            total = total * mask[h, rows, :].reshape(chunk, 1, HALF)
             moment = ADAM_BETA * mom[h, rows] + (1.0 - ADAM_BETA) * total * total
             summed[h][rows] = total
             mom_out[h, rows] = moment
@@ -142,12 +144,12 @@
         for d in Z_ORDER:
             there = lax.rem(my_z + d, NZ)
             target = zr[h][0] if d == 0 else zsb.at[h, d - 1]
-            base = there * cap
+            base = there * FULL
 
             @pl.loop(0, cap, step=8)
             def _(k0):
                 for u in range(8):
-                    target[k0 + u] = summed[h][zpack[base + k0 + u]]
+                    target[k0 + u] = summed[h][table[0, base + k0 + u]]
 
             target[cap] = adam
             if d:
@@ -168,7 +170,7 @@
                 base = yc_index(e) * SLOTS
                 target = ysb.at[h, e - 1, d] if e else yr.at[h, my_yc, source_z]
                 for j in range(SLOTS):
-                    target[j] = zr[h][d][ypack[base + j]]
+                    target[j] = zr[h][d][table[1, base + j]]
                 target[SLOTS] = zr[h][d][cap]
                 if e:
                     pltpu.make_async_remote_copy(
@@ -192,7 +194,7 @@
             y, zs = lax.div(t, NZ), lax.rem(t, NZ)
             for j in range(SLOTS):
                 tile = jnp.concatenate([yr[h, y * NC, zs, j], yr[h, y * NC + 1, zs, j]], axis=0)
-                tile = jnp.where(own_info[j] > 0, tile, 0.0)
+                tile = jnp.where(table[5, j] > 0, tile, 0.0)
                 gfull[j, pl.ds(pl.multiple_of(t * 8, 8), 8), h * HALF:(h + 1) * HALF] = tile
             return total + (yr[h, y * NC, zs, SLOTS] + yr[h, y * NC + 1, zs, SLOTS])
 
@@ -210,7 +212,7 @@
         inner = dot(lroot[j], high) + dot(lroot[j], low)
         in_high, in_low = split(inner)
         prec = dot(in_high, rroot[j]) + dot(in_low, rroot[j])
-        live = (row_ids < own_info[8 + j] * HALF) & (col_ids < own_info[16 + j] * HALF)
+        live = (row_ids < table[6, j] * HALF) & (col_ids < table[7, j] * HALF)
         prec = jnp.where(live, prec, 0.0)
         prec_sq = jnp.sum(prec * prec)
         adam_sq = jnp.sum(own_hot[pl.ds(j, 1), :] * adam_row)
@@ -246,7 +248,7 @@
         @pl.loop(0, cap, step=8)
         def _(k0):
             for u in range(8):
-                target[k0 + u] = ybr[d][bpack[k0 + u]]
+                target[k0 + u] = ybr[d][table[2, k0 + u]]
 
         if d:
             copy = pltpu.make_async_remote_copy(
@@ -282,7 +284,7 @@
     @pl.loop(0, COLUMN, step=8)
     def _(b0):
         for u in range(8):
-            new_w[b0 + u] = wbuf[b0 + u] - zbr[home[b0 + u]]
+            new_w[b0 + u] = wbuf[b0 + u] - zbr[table[3, b0 + u] * cap + table[4, b0 + u]]
 
     for h in range(2):
         for copy in rs[h]:
@@ -301,41 +303,97 @@
         copy.wait()
 
 
-def tables(owner, extent, cap):
-    me = lax.axis_index("fsdp").astype(jnp.int32)
-    my_z = (me // NC) % NZ
-    ids = jnp.arange(COLUMN, dtype=jnp.int32)
-    plane = (owner // NC) % NZ
-    yc = (owner // (NC * NZ)) * NC + owner % NC
-    before = ids[None, :] < ids[:, None]
-    rank_owner = jnp.sum((before & (owner[None, :] == owner[:, None])).astype(jnp.int32), axis=1)
-    rank_plane = jnp.sum((before & (plane[None, :] == plane[:, None])).astype(jnp.int32), axis=1)
-    home = plane * cap + rank_plane
-    slot = yc * SLOTS + rank_owner
-
-    def invert(keys, size, values):
-        hits = keys[None, :] == jnp.arange(size, dtype=jnp.int32)[:, None]
-        return jnp.sum(jnp.where(hits, values[None, :], 0), axis=1)
-
+def plan_kernel(owner, extent, table, mask, own_hot, need, mine, theirs, send_sem, recv_sem):
+    me = lax.axis_index("fsdp")
+    my_x = lax.axis_index("tp")
+    my_z = lax.rem(lax.div(me, NC), NZ)
+    barrier = pltpu.get_barrier_semaphore()
+    peers = [{"tp": lax.rem(my_x + d, NX)} for d in range(1, NX)]
+    for peer in peers:
+        pl.semaphore_signal(barrier, inc=1, device_id=peer, device_id_type=MESH)
+
+    def down(row):
+        return jnp.broadcast_to(row.astype(F32), (COLUMN, COLUMN)).T.astype(jnp.int32)
+
+    own = owner[...]
+    plane = lax.rem(lax.div(own, NC), NZ)
+    own_t, plane_t = down(own), down(plane)
+    earlier = lax.broadcasted_iota(jnp.int32, (COLUMN, COLUMN), 0) < lax.broadcasted_iota(jnp.int32, (COLUMN, COLUMN), 1)
+
+    def rank(keys, keys_t):
+        same = earlier & (keys_t == keys)
+        return jnp.sum(jnp.where(same, 1.0, 0.0), axis=0, keepdims=True).astype(jnp.int32)
+
+    rank_plane = rank(plane, plane_t)
+    mine[...] = jnp.broadcast_to(jnp.max(rank_plane.astype(F32), axis=1, keepdims=True) + 1.0, (8, COLUMN))
+    pl.semaphore_wait(barrier, len(peers))
+    copies = []
+    for d, peer in enumerate(peers):
+        copy = pltpu.make_async_remote_copy(
+            src_ref=mine, dst_ref=theirs.at[d], send_sem=send_sem.at[d], recv_sem=recv_sem.at[d],
+            device_id=peer, device_id_type=MESH,
+        )
+        copy.start()
+        copies.append(copy)
+
+    rank_owner = rank(own, own_t)
+    slot = (lax.div(own, NC * NZ) * NC + lax.rem(own, NC)) * SLOTS + rank_owner
+    ids_t = lax.broadcasted_iota(jnp.int32, (COLUMN, COLUMN), 0)
+    lanes = lax.broadcasted_iota(jnp.int32, (COLUMN, COLUMN), 1)
+    zero = jnp.zeros((1, COLUMN), jnp.int32)
+
+    def invert(keys_t, start, values_t):
+        hits = keys_t == lanes + start
+        return jnp.sum(jnp.where(hits, values_t.astype(F32), 0.0), axis=0, keepdims=True).astype(jnp.int32)
+
+    home_t = down(plane * FULL + rank_plane)
+    for i in range(NZ * FULL // COLUMN):
+        table[0:1, i * COLUMN:(i + 1) * COLUMN] = invert(home_t, i * COLUMN, ids_t)
     here = plane == my_z
-    zpack = invert(home, NZ * cap, ids)
-    ypack = invert(jnp.where(here, slot, -1), NYC * SLOTS, rank_plane)
-    bpack = invert(jnp.where(here, rank_plane, -1), cap, slot)
-    mine = jnp.where(owner == me, rank_owner, -1)
-    own_hot = (mine[None, :] == jnp.arange(8, dtype=jnp.int32)[:, None])
-    own_info = jnp.concatenate([
-        jnp.sum(own_hot.astype(jnp.int32), axis=1),
-        jnp.sum(jnp.where(own_hot, extent[None, :, 0], 0), axis=1),
-        jnp.sum(jnp.where(own_hot, extent[None, :, 1], 0), axis=1),
-    ])
-    row_live = me * 4 < extent[:, 0] * HALF
-    col_live = jnp.arange(2, dtype=jnp.int32)[:, None] < extent[None, :, 1]
-    live = (row_live[None, :] & col_live).astype(F32)
-    mask = jnp.broadcast_to(live[:, :, None, None], (2, COLUMN, 1, HALF))
-    return zpack, ypack, bpack, home, own_info, mask, own_hot.astype(F32)
-
-
-def run_step(cap, grads, weights, moments, left_stat, right_stat, left_root, right_root, owner, extent):
+    slot_t, rank_t = down(slot), down(rank_plane)
+    mine_t = down(jnp.where(own == me, rank_owner, -1))
+    table[1:2, 0:COLUMN] = invert(down(jnp.where(here, slot, -1)), 0, rank_t)
+    table[2:3, 0:COLUMN] = invert(down(jnp.where(here, rank_plane, -1)), 0, slot_t)
+    table[3:4, 0:COLUMN] = plane
+    table[4:5, 0:COLUMN] = rank_plane
+    table[5:6, 0:COLUMN] = invert(mine_t, 0, jnp.ones_like(ids_t))
+    rows, cols = extent[0:1, :], extent[1:2, :]
+    table[6:7, 0:COLUMN] = invert(mine_t, 0, down(rows))
+    table[7:8, 0:COLUMN] = invert(mine_t, 0, down(cols))
+    row_live = me * 4 < rows * HALF
+    for h in range(2):
+        mask[h] = down(jnp.where(row_live & (h < cols), 1, 0)).astype(F32)
+    here_slot = jnp.broadcast_to(jnp.where(own == me, rank_owner, -1), (8, COLUMN))
+    own_hot[...] = jnp.where(here_slot == lax.broadcasted_iota(jnp.int32, (8, COLUMN), 0), 1.0, 0.0)
+    for copy in copies:
+        copy.wait_recv()
+    need[...] = jnp.maximum(jnp.maximum(mine[...], theirs[0]), jnp.maximum(theirs[1], theirs[2]))
+    for copy in copies:
+        copy.wait_send()
+
+
+def make_plan(owner, extent):
+    vmem = pl.BlockSpec(memory_space=pltpu.VMEM)
+    return pl.pallas_call(
+        plan_kernel,
+        out_shape=(
+            jax.ShapeDtypeStruct((8, NZ * FULL), jnp.int32),
+            jax.ShapeDtypeStruct((2, COLUMN, HALF), F32),
+            jax.ShapeDtypeStruct((8, COLUMN), F32),
+            jax.ShapeDtypeStruct((8, COLUMN), F32),
+        ),
+        in_specs=[vmem] * 2,
+        out_specs=(vmem,) * 4,
+        scratch_shapes=[
+            pltpu.VMEM((8, COLUMN), F32), pltpu.VMEM((NX - 1, 8, COLUMN), F32),
+            pltpu.SemaphoreType.DMA((NX - 1,)), pltpu.SemaphoreType.DMA((NX - 1,)),
+        ],
+        compiler_params=pltpu.CompilerParams(collective_id=0, has_side_effects=True),
+        name="plan",
+    )(owner.reshape(1, COLUMN), extent.T)
+
+
+def run_step(cap, table, mask, own_hot, grads, moments, weights, left_stat, right_stat, left_root, right_root):
     piece = (4, HALF)
     any_spec = pl.BlockSpec(memory_space=pl.ANY)
     smem = pl.BlockSpec(memory_space=pltpu.SMEM)
@@ -373,7 +431,7 @@
         ]
     )
     halves = lambda a: a.reshape(-1, 4, 2, HALF).transpose(0, 2, 1, 3)
-    zpack, ypack, bpack, home, own_info, mask, own_hot = tables(owner, extent, cap)
+    whole = lambda a: a.reshape(COLUMN, 2, 4, HALF).transpose(0, 2, 1, 3).reshape(COLUMN, 4, size)
     new_w, new_m, new_left, new_right = pl.pallas_call(
         functools.partial(step_kernel, cap),
         out_shape=(
@@ -382,24 +440,29 @@
             jax.ShapeDtypeStruct((SLOTS, size, size), F32),
             jax.ShapeDtypeStruct((SLOTS, size, size), F32),
         ),
-        in_specs=[smem] * 5 + [vmem] * 2 + [any_spec] * 7,
+        in_specs=[smem] + [vmem] * 2 + [any_spec] * 7,
         out_specs=(vmem, any_spec, any_spec, any_spec),
         scratch_shapes=scratch,
         compiler_params=pltpu.CompilerParams(
-            collective_id=0, has_side_effects=True, vmem_limit_bytes=48 * 1024 * 1024
+            collective_id=1 + CAPS.index(cap), has_side_effects=True, vmem_limit_bytes=62 * 1024 * 1024
         ),
         name="step",
     )(
-        zpack, ypack, bpack, home, own_info, mask, own_hot,
+        table, mask, own_hot,
         halves(grads[0]), halves(moments), halves(weights).reshape(COLUMN, 8, HALF),
         left_stat[0, 0], right_stat[0, 0], left_root[0, 0], right_root[0, 0],
     )
-    whole = lambda a: a.reshape(COLUMN, 2, 4, HALF).transpose(0, 2, 1, 3).reshape(COLUMN, 4, size)
     return whole(new_w), whole(new_m), new_left[None, None], new_right[None, None]
 
 
-def on_device(*args):
-    return run_step(NYC * SLOTS, *args)
+def on_device(grads, weights, moments, left_stat, right_stat, left_root, right_root, owner, extent):
+    table, mask, own_hot, need = make_plan(owner, extent)
+    return lax.cond(
+        need[0, 0] <= CAPS[0],
+        functools.partial(run_step, CAPS[0]),
+        functools.partial(run_step, CAPS[1]),
+        table, mask, own_hot, grads, moments, weights, left_stat, right_stat, left_root, right_root,
+    )
 
 
 def solution(mesh):

time: 129 us -> 113 us (0.88)
  Pallas kernels: 115 us -> 104 us
  other arithmetic: 2.94 us -> 0 us
  local copies, waits for them, and re-layouts: 10.1 us -> 8.05 us
    pallas_call x1, Pallas kernels: 115 us -> 96.6 us  [run_step(): pl.pallas_call(functools.partial(step_kernel, cap), out_shape=(jax.ShapeD...]
    pallas_call x0 -> x1, Pallas kernels: none -> 7.02 us  [make_plan(): pl.pallas_call(plan_kernel, out_shape=(jax.ShapeDtypeStruct((8, NZ * FULL...]
    unnamed x14 -> x6, local copies, waits for them, and re-layouts: 9.05 us -> 6.85 us
    reduce_sum x5 -> x0, other arithmetic: 1.48 us -> none  [the longest x1 0.9 us: tables(): jnp.sum((before & (owner[None, :] == owner[:, None])).astype(jnp.int32),...]
where the time goes in v3:
time: 113 us
  Pallas kernels  104 us (92%)
  local copies, waits for them, and re-layouts  8.05 us (7%)
  between operations  1.3 us (1%)
    pallas_call x1, Pallas kernels, run_step(): pl.pallas_call(functools.partial(step_kernel, cap), out_shape=(jax.ShapeD...  96.6 us
    pallas_call x1, Pallas kernels, make_plan(): pl.pallas_call(plan_kernel, out_shape=(jax.ShapeDtypeStruct((8, NZ * FULL...  7.02 us
    unnamed x6, local copies, waits for them, and re-layouts  6.85 us

profile of v3, /device:TPU:1, one launch (start us, length us, event | category | flops | bytes accessed | tf_op | source)
XLA Modules:
  0.0 113.0 jit_solution(9699985024361249841)
XLA Ops:
  0.6 7.0 %plan.1 = (s32[8,384]{1,0:T(8,128)S(1)}, f32[2,128,128]{2,1,0:T(8,128)S(1)}, f32[8,128]{1,0:T(8,128)S(1)}, f32[8,128]{1,0:T(8,128)}) custom-call(s32[1,128]{1,0:T(1,128)} %bitcast.76, s32[2,128]{1,0:T(2,128)} %bitcast.75), custom_call_target="tpu_custom_call" | custom-call | tf_op jit(solution)/shard_map/plan/pallas_call | solution.py:377
  7.7 1.2 %slice.3 = f32[1,1]{1,0:T(1,128)} slice(f32[8,128]{1,0:T(8,128)} %get-tuple-element.76), slice={[0:1], [0:1]} | slice | bytes 8 | tf_op jit(solution)/shard_map/slice | solution.py:461
  9.5 96.6 %conditional.1 = (f32[128,4,256]{2,1,0:T(4,128)}, f32[128,4,256]{2,1,0:T(4,128)}, f32[1,1,6,256,256]{4,3,2,1,0:T(8,128)S(1)}, f32[1,1,6,256,256]{4,3,2,1,0:T(8,128)}) conditional(s32[]{:T(128)} %bitcast.52, (f32[1,512,4,256]{3,2,1,0:T(4,128)}, f32[128,4,256]{2,1,0:T(4,128)}, f32[128,4,256]{2,1,0:T(4,128)}, f32[1,1,6,256,256]{4,3,2,1,0:T(8,128)}, ...), branch_computations={%region_0.0_spmd, %region_1.0_spmd} | conditional | bytes 32 | solution.py:460
  9.5 96.6 %step.3 = (f32[128,8,128]{2,1,0:T(8,128)}, f32[128,2,4,128]{3,2,1,0:T(4,128)}, f32[6,256,256]{2,1,0:T(8,128)S(1)}, f32[6,256,256]{2,1,0:T(8,128)}) custom-call(s32[8,384]{1,0:T(8,128)S(1)} %get-tuple-element.54.table, f32[2,128,128]{2,1,0:T(8,128)S(1)} %get-tuple-element.55.mask, f32[8,128]{1,0:T(8,128)S(1)} %get-tuple-element.56.own_hot, ...), custom_call_target="tpu_custom_call" | custom-call | tf_op jit(solution)/shard_map/cond/branch_1_fun/step/pallas_call | solution.py:435
  106.1 1.9 %copy.35 = f32[128,4,256]{2,1,0:T(4,128)} copy(f32[128,4,256]{2,1,0:T(4,128)} %get-tuple-element.96) | data formatting | bytes 1048576
  108.0 1.9 %copy.36 = f32[128,4,256]{2,1,0:T(4,128)} copy(f32[128,4,256]{2,1,0:T(4,128)} %get-tuple-element.97) | data formatting | bytes 1048576
  109.8 0.0 copy-start
  109.8 1.1 %copy.37 = f32[1,1,6,256,256]{4,3,2,1,0:T(8,128)} copy(f32[1,1,6,256,256]{4,3,2,1,0:T(8,128)S(1)} %get-tuple-element.98) | data formatting | bytes 3145728
  111.0 0.8 copy-done
  111.8 1.1 %copy.38 = f32[1,1,6,256,256]{4,3,2,1,0:T(8,128)} copy(f32[1,1,6,256,256]{4,3,2,1,0:T(8,128)S(1)} %copy-done) | data formatting | bytes 3145728
Async XLA Ops:
  109.8 2.0 %copy-start = (f32[1,1,6,256,256]{4,3,2,1,0:T(8,128)S(1)}, f32[1,1,6,256,256]{4,3,2,1,0:T(8,128)}, u32[]{:S(2)}) copy-start(f32[1,1,6,256,256]{4,3,2,1,0:T(8,128)} %get-tuple-element.99) | copy-start | bytes 4718596

commit v4 on v3

v4 whole, which is shorter than its diff:
```python
import functools

import jax
import jax.numpy as jnp
from jax import lax
from jax.experimental import pallas as pl
from jax.experimental.pallas import tpu as pltpu
from jax.sharding import PartitionSpec as P

ADAM_BETA = 0.95
STAT_BETA = 0.99
LEARN_RATE = 0.05
ADAM_EPS = 1e-08
NORM_EPS = 1e-06

NX, NY, NZ, NC = 4, 4, 8, 2
NYC = NY * NC
COLUMN = 128
SLOTS = 6
HALF = 128
FULL = NYC * SLOTS
EARLY = 2
FIRST = NYC * EARLY
CAPS = (28, 32, FULL)
MESH = pl.DeviceIdType.MESH
Z_ORDER = (4, 3, 5, 2, 6, 1, 7, 0)
F32 = jnp.float32
BF16 = jnp.bfloat16


def split(value):
    high = value.astype(BF16)
    low = (value - high.astype(F32)).astype(BF16)
    return high, low


def dot(a, b, dims=((1,), (0,))):
    return lax.dot_general(a, b, (dims, ((), ())), preferred_element_type=F32)


def units(cap):
    return (
        (0, 0, SLOTS, 1, 0, cap),
        (1, 0, EARLY, 1, 0, FIRST),
        (1, EARLY, SLOTS, 0, FIRST, cap),
    )


PARTS = ((0, EARLY), (EARLY, SLOTS))


def step_kernel(
    cap,
    table, mask, own_hot, grads, moments, weights, left, right, left_root, right_root,
    new_w, new_m, new_left, new_right,
    *scratch,
):
    scratch = list(scratch)
    unit = units(cap)
    zr = [[scratch.pop(0) for _ in range(NZ)] for _ in unit]
    zsb = [scratch.pop(0) for _ in unit]
    ysb = [scratch.pop(0) for _ in unit]
    yr = [scratch.pop(0) for _ in unit]
    ybr = [[scratch.pop(0) for _ in range(NZ)] for _ in PARTS]
    ybs = [scratch.pop(0) for _ in PARTS]
    zbs = [scratch.pop(0) for _ in PARTS]
    summed = [scratch.pop(0) for _ in range(2)]
    (own_part, parts, mom, mom_out, arow, gfull, lroot, rroot, lstat, rstat, zbr, wbuf,
     rs_send, rs_recv, z_send, z_recv, y_send, y_recv, yb_send, yb_recv, zb_send, zb_recv,
     loc_sem, in_sem, out_sem) = scratch

    me = lax.axis_index("fsdp")
    my_x = lax.axis_index("tp")
    my_c = lax.rem(me, NC)
    my_z = lax.rem(lax.div(me, NC), NZ)
    my_y = lax.div(me, NC * NZ)
    my_yc = my_y * NC + my_c

    def index_of(y, z, c):
        return (y * NZ + z) * NC + c

    def z_peer(d):
        return {"fsdp": index_of(my_y, lax.rem(my_z + d, NZ), my_c)}

    def yc_at(e):
        return lax.rem(my_y + e // NC, NY), lax.rem(my_c + e % NC, NC)

    def yc_peer(e):
        y, c = yc_at(e)
        return {"fsdp": index_of(y, my_z, c)}

    def yc_index(e):
        y, c = yc_at(e)
        return y * NC + c

    def x_peer(d):
        return {"tp": lax.rem(my_x + d, NX)}

    def remote(source, target, send, recv, peer):
        return pltpu.make_async_remote_copy(
            src_ref=source, dst_ref=target, send_sem=send, recv_sem=recv, device_id=peer, device_id_type=MESH
        )

    barrier = pltpu.get_barrier_semaphore()
    peers = [x_peer(d) for d in range(1, NX)] + [z_peer(d) for d in range(1, NZ)] + [yc_peer(e) for e in range(1, NYC)]
    for peer in peers:
        pl.semaphore_signal(barrier, inc=1, device_id=peer, device_id_type=MESH)
    own_copies = [
        pltpu.make_async_copy(grads.at[pl.ds(my_x * COLUMN, COLUMN), h], own_part.at[h], loc_sem.at[h]) for h in range(2)
    ]
    mom_copies = [pltpu.make_async_copy(moments.at[:, h], mom.at[h], loc_sem.at[2 + h]) for h in range(2)]
    for copy in own_copies + mom_copies:
        copy.start()
    pl.semaphore_wait(barrier, len(peers))

    rs = []
    for h in range(2):
        row = []
        for d in (2, 1, 3):
            there = lax.rem(my_x + d, NX)
            copy = remote(
                grads.at[pl.ds(there * COLUMN, COLUMN), h], parts.at[h, d - 1],
                rs_send.at[h, d - 1], rs_recv.at[h, d - 1], x_peer(d),
            )
            copy.start()
            row.append(copy)
        rs.append(row)
    big_in = [
        pltpu.make_async_copy(left_root, lroot, in_sem.at[0]),
        pltpu.make_async_copy(right_root, rroot, in_sem.at[1]),
        pltpu.make_async_copy(left, lstat, in_sem.at[2]),
        pltpu.make_async_copy(right, rstat, in_sem.at[3]),
        pltpu.make_async_copy(weights, wbuf, in_sem.at[4]),
    ]
    for copy in big_in:
        copy.start()

    chunk = 8
    out_copies = []

    def sum_half(h):
        own_copies[h].wait()
        mom_copies[h].wait()
        for copy in rs[h]:
            copy.wait_recv()

        @pl.loop(0, COLUMN // chunk)
        def _(i):
            rows = pl.ds(i * chunk, chunk)
            total = (own_part[h, rows] + parts[h, 0, rows]) + (parts[h, 1, rows] + parts[h, 2, rows])
            total = total * mask[h, rows, :].reshape(chunk, 1, HALF)
            moment = ADAM_BETA * mom[h, rows] + (1.0 - ADAM_BETA) * total * total
            summed[h][rows] = total
            mom_out[h, rows] = moment
            direction = total / (jnp.sqrt(moment) + ADAM_EPS)
            arow[rows, :] = jnp.sum(direction * direction, axis=1)

        out_copy = pltpu.make_async_copy(mom_out.at[h], new_m.at[:, h], out_sem.at[h])
        out_copy.start()
        out_copies.append(out_copy)
        return lax.dot_general(
            jnp.ones((8, COLUMN), F32), arow[...], (((1,), (1,)), ((), ())),
            precision=lax.Precision.HIGHEST, preferred_element_type=F32,
        )[0:4]

    def z_out(u, adam):
        h, _, _, with_adam, low, high = unit[u]
        copies = [None] * NZ
        for d in Z_ORDER:
            target = zsb[u].at[d - 1] if d else zr[u][0]
            base = lax.rem(my_z + d, NZ) * FULL + low

            @pl.loop(0, high - low, step=4)
            def _(k0):
                for i in range(4):
                    target[k0 + i] = summed[h][table[0, base + k0 + i]]

            if with_adam:
                target[high - low] = adam
            if d:
                copies[d] = remote(zsb[u].at[d - 1], zr[u][d], z_send.at[u, d - 1], z_recv.at[u, d - 1], z_peer(d))
                copies[d].start()
        return copies

    def y_out(u):
        _, first, last, with_adam, low, high = unit[u]
        for d in (0,) + Z_ORDER[:-1]:
            if d:
                z_copies[u][d].wait_recv()
            source_z = lax.rem(my_z + (NZ - d), NZ)
            for e in range(NYC):
                base = yc_index(e) * SLOTS
                there = yr[u].at[my_yc, source_z]
                target = ysb[u].at[e - 1, d] if e else there
                for j in range(first, last):
                    index = table[1, base + j]
                    target[j - first] = zr[u][d][jnp.maximum(index - low, 0) if low else index]
                if with_adam:
                    target[last - first] = zr[u][d][high - low]
                if e:
                    remote(ysb[u].at[e - 1, d], there, y_send.at[u], y_recv.at[u], yc_peer(e)).start()

    def y_all(u):
        return remote(ysb[u], yr[u].at[pl.ds(0, NYC - 1)], y_send.at[u], y_recv.at[u], yc_peer(1))

    def build(u, total):
        h, first, last, with_adam, _, _ = unit[u]
        y_all(u).wait_recv()

        def body(t, total):
            y, zs = lax.div(t, NZ), lax.rem(t, NZ)
            for j in range(first, last):
                tile = jnp.concatenate([yr[u][y * NC, zs, j - first], yr[u][y * NC + 1, zs, j - first]], axis=0)
                tile = jnp.where(table[5, j] > 0, tile, 0.0)
                gfull[j, pl.ds(pl.multiple_of(t * 8, 8), 8), h * HALF:(h + 1) * HALF] = tile
            if with_adam:
                total = total + (yr[u][y * NC, zs, last - first] + yr[u][y * NC + 1, zs, last - first])
            return total

        return lax.fori_loop(0, NY * NZ, body, total)

    row_ids = lax.broadcasted_iota(jnp.int32, (2 * HALF, 2 * HALF), 0)
    col_ids = lax.broadcasted_iota(jnp.int32, (2 * HALF, 2 * HALF), 1)

    def precondition(p, adam_row):
        first, last = PARTS[p]

        @pl.loop(first, last)
        def _(j):
            high, low = split(gfull[j])
            inner = dot(lroot[j], high) + dot(lroot[j], low)
            in_high, in_low = split(inner)
            prec = dot(in_high, rroot[j]) + dot(in_low, rroot[j])
            live = (row_ids < table[6, j] * HALF) & (col_ids < table[7, j] * HALF)
            prec = jnp.where(live, prec, 0.0)
            prec_sq = jnp.sum(prec * prec)
            adam_sq = jnp.sum(own_hot[pl.ds(j, 1), :] * adam_row)
            graft = LEARN_RATE * jnp.sqrt(jnp.full((1, HALF), adam_sq) / (jnp.full((1, HALF), prec_sq) + NORM_EPS))
            left_cols = (prec[:, :HALF] * graft).reshape(NY * NZ, 8, HALF)
            right_cols = (prec[:, HALF:] * graft).reshape(NY * NZ, 8, HALF)
            for core in range(NC):
                rows = slice(core * 4, core * 4 + 4)
                piece = jnp.concatenate([left_cols[:, rows], right_cols[:, rows]], axis=1)
                for y in range(NY):
                    ybs[p][y * NC + core, :, j - first] = piece[y * NZ:(y + 1) * NZ]

        count = last - first
        for d in Z_ORDER:
            dest_z = lax.rem(my_z + d, NZ)
            for e in range(1, NYC):
                remote(
                    ybs[p].at[yc_index(e), dest_z], ybr[p][d].at[pl.ds(my_yc * count, count)],
                    yb_send.at[p], yb_recv.at[p, d], yc_peer(e),
                ).start()

    zb_copies = []

    def z_back(p):
        first, last = PARTS[p]
        count = last - first
        low, high = (0, FIRST) if p == 0 else (FIRST, cap)
        here = zbr.at[pl.ds(my_z * cap + low, high - low)]
        for d in Z_ORDER:
            dest_z = lax.rem(my_z + d, NZ)
            ybr[p][d][pl.ds(my_yc * count, count)] = ybs[p][my_yc, dest_z]
            arrived = ybr[p][d].at[pl.ds(0, (NYC - 1) * count)]
            remote(arrived, arrived, yb_send.at[p], yb_recv.at[p, d], yc_peer(1)).wait_recv()
            target = zbs[p].at[d - 1] if d else here

            @pl.loop(0, high - low, step=4)
            def _(k0):
                for i in range(4):
                    target[k0 + i] = ybr[p][d][table[2, low + k0 + i]]

            if d:
                copy = remote(zbs[p].at[d - 1], here, zb_send.at[p, d - 1], zb_recv.at[p, d - 1], z_peer(d))
                copy.start()
                zb_copies.append(copy)

    adam = sum_half(0)
    z_copies = [z_out(0, adam)]
    adam = sum_half(1)
    z_copies += [z_out(1, adam), z_out(2, adam)]
    y_out(0)
    y_out(1)
    adam_total = build(0, jnp.zeros((4, COLUMN), F32))
    adam_row = build(1, adam_total)[0:1]
    big_in[0].wait()
    big_in[1].wait()
    precondition(0, adam_row)
    y_out(2)
    z_back(0)
    build(2, adam_total)
    precondition(1, adam_row)
    z_back(1)

    big_in[2].wait()
    big_in[3].wait()

    @pl.loop(0, SLOTS)
    def _(j):
        high, low = split(gfull[j])
        rows = ((1,), (1,))
        outer = dot(high, high, rows) + (dot(high, low, rows) + dot(low, high, rows))
        lstat[j] = STAT_BETA * lstat[j] + (1.0 - STAT_BETA) * outer
        cols = ((0,), (0,))
        outer = dot(high, high, cols) + (dot(high, low, cols) + dot(low, high, cols))
        rstat[j] = STAT_BETA * rstat[j] + (1.0 - STAT_BETA) * outer

    for i, (source, out) in enumerate(((lstat, new_left), (rstat, new_right))):
        out_copy = pltpu.make_async_copy(source, out, out_sem.at[2 + i])
        out_copy.start()
        out_copies.append(out_copy)

    big_in[4].wait()
    for copy in zb_copies:
        copy.wait_recv()

    @pl.loop(0, COLUMN, step=8)
    def _(b0):
        for i in range(8):
            new_w[b0 + i] = wbuf[b0 + i] - zbr[table[3, b0 + i] * cap + table[4, b0 + i]]

    for h in range(2):
        for copy in rs[h]:
            copy.wait_send()
    for u in range(len(unit)):
        for d in range(1, NZ):
            z_copies[u][d].wait_send()
        y_all(u).wait_send()
    for p in range(len(PARTS)):
        sent = ybs[p].at[pl.ds(0, NYC - 1)]
        remote(sent, sent, yb_send.at[p], yb_recv.at[p, 0], yc_peer(1)).wait_send()
    for copy in zb_copies:
        copy.wait_send()
    for copy in out_copies:
        copy.wait()


def plan_kernel(owner, extent, choice, table, mask, own_hot, mine, theirs, send_sem, recv_sem):
    me = lax.axis_index("fsdp")
    my_z = lax.rem(lax.div(me, NC), NZ)
    my_x = lax.axis_index("tp")
    barrier = pltpu.get_barrier_semaphore()
    peers = [{"tp": lax.rem(my_x + d, NX)} for d in range(1, NX)]
    for peer in peers:
        pl.semaphore_signal(barrier, inc=1, device_id=peer, device_id_type=MESH)
    owners = NYC * NZ
    owner_ids = lax.broadcasted_iota(jnp.int32, (owners, COLUMN), 0)
    owned = jnp.where(jnp.broadcast_to(owner[...], (owners, COLUMN)) == owner_ids, 1.0, 0.0)
    excess = jnp.maximum(jnp.sum(owned, axis=1, keepdims=True) - EARLY, 0.0)
    in_plane = lax.rem(lax.div(owner_ids, NC), NZ) == lax.broadcasted_iota(jnp.int32, (owners, COLUMN), 1)
    late_blocks = jnp.sum(jnp.where(in_plane, excess, 0.0), axis=0, keepdims=True)
    mine[...] = jnp.broadcast_to(late_blocks + FIRST, (8, COLUMN))
    pl.semaphore_wait(barrier, len(peers))
    copies = []
    for d, peer in enumerate(peers):
        copy = pltpu.make_async_remote_copy(
            src_ref=mine, dst_ref=theirs.at[d], send_sem=send_sem.at[d], recv_sem=recv_sem.at[d],
            device_id=peer, device_id_type=MESH,
        )
        copy.start()
        copies.append(copy)
    fill_tables(me, my_z, owner, extent, table, mask, own_hot)
    for copy in copies:
        copy.wait_recv()
    need = jnp.max(jnp.maximum(jnp.maximum(mine[...], theirs[0]), jnp.maximum(theirs[1], theirs[2])))
    index = jnp.int32(0)
    for cap in CAPS[:-1]:
        index = index + jnp.where(need > cap, jnp.int32(1), jnp.int32(0))
    choice[0, 0] = index
    for copy in copies:
        copy.wait_send()


def make_plan(owner, extent):
    vmem = pl.BlockSpec(memory_space=pltpu.VMEM)
    return pl.pallas_call(
        plan_kernel,
        out_shape=(
            jax.ShapeDtypeStruct((1, 1), jnp.int32),
            jax.ShapeDtypeStruct((8, NZ * FULL), jnp.int32),
            jax.ShapeDtypeStruct((2, COLUMN, HALF), F32),
            jax.ShapeDtypeStruct((8, COLUMN), F32),
        ),
        in_specs=[vmem] * 2,
        out_specs=(pl.BlockSpec(memory_space=pltpu.SMEM), vmem, vmem, vmem),
        scratch_shapes=[
            pltpu.VMEM((8, COLUMN), F32), pltpu.VMEM((NX - 1, 8, COLUMN), F32),
            pltpu.SemaphoreType.DMA((NX - 1,)), pltpu.SemaphoreType.DMA((NX - 1,)),
        ],
        compiler_params=pltpu.CompilerParams(collective_id=0, has_side_effects=True),
        name="plan",
    )(owner, extent)


def fill_tables(me, my_z, owner, extent, table, mask, own_hot):
    def down(row):
        return jnp.broadcast_to(row.astype(F32), (COLUMN, COLUMN)).T.astype(jnp.int32)

    own = owner[...]
    plane = lax.rem(lax.div(own, NC), NZ)
    own_t = down(own)
    ids_t = lax.broadcasted_iota(jnp.int32, (COLUMN, COLUMN), 0)
    lanes = lax.broadcasted_iota(jnp.int32, (COLUMN, COLUMN), 1)
    earlier = ids_t < lanes

    def rank(keys, keys_t):
        same = earlier & (keys_t == keys)
        return jnp.sum(jnp.where(same, 1.0, 0.0), axis=0, keepdims=True).astype(jnp.int32)

    def invert(keys_t, start, values_t):
        hits = keys_t == lanes + start
        return jnp.sum(jnp.where(hits, values_t.astype(F32), 0.0), axis=0, keepdims=True).astype(jnp.int32)

    rank_owner = rank(own, own_t)
    late = jnp.where(rank_owner >= EARLY, 1, 0)
    key = plane * 2 + late
    rank_plane = rank(key, down(key)) + late * FIRST
    yc = lax.div(own, NC * NZ) * NC + lax.rem(own, NC)
    slot = yc * SLOTS + rank_owner
    slot_in_part = jnp.where(late > 0, yc * (SLOTS - EARLY) + rank_owner - EARLY, yc * EARLY + rank_owner)
    home_t = down(plane * FULL + rank_plane)
    for i in range(NZ * FULL // COLUMN):
        table[0:1, i * COLUMN:(i + 1) * COLUMN] = invert(home_t, i * COLUMN, ids_t)
    here = plane == my_z
    rank_t = down(rank_plane)
    mine = jnp.where(own == me, rank_owner, -1)
    mine_t = down(mine)
    table[1:2, 0:COLUMN] = invert(down(jnp.where(here, slot, -1)), 0, rank_t)
    table[2:3, 0:COLUMN] = invert(down(jnp.where(here, rank_plane, -1)), 0, down(slot_in_part))
    table[3:4, 0:COLUMN] = plane
    table[4:5, 0:COLUMN] = rank_plane
    table[5:6, 0:COLUMN] = invert(mine_t, 0, jnp.ones_like(ids_t))
    rows, cols = extent[0:1, :], extent[1:2, :]
    table[6:7, 0:COLUMN] = invert(mine_t, 0, down(rows))
    table[7:8, 0:COLUMN] = invert(mine_t, 0, down(cols))
    row_live = me * 4 < rows * HALF
    for h in range(2):
        mask[h] = down(jnp.where(row_live & (h < cols), 1, 0)).astype(F32)
    here_slot = jnp.broadcast_to(mine, (8, COLUMN))
    own_hot[...] = jnp.where(here_slot == lax.broadcasted_iota(jnp.int32, (8, COLUMN), 0), 1.0, 0.0)


def run_step(cap, table, mask, own_hot, grads, moments, weights, left_stat, right_stat, left_root, right_root):
    piece = (4, HALF)
    any_spec = pl.BlockSpec(memory_space=pl.ANY)
    hbm = pl.BlockSpec(memory_space=pltpu.HBM)
    vmem = pl.BlockSpec(memory_space=pltpu.VMEM)
    size = 2 * HALF
    dma = pltpu.SemaphoreType.DMA
    unit = units(cap)
    pieces = [high - low + with_adam for _, _, _, with_adam, low, high in unit]
    slots = [last - first + with_adam for _, first, last, with_adam, _, _ in unit]
    part_slots = [last - first for first, last in PARTS]
    home_pieces = [FIRST, cap - FIRST]
    scratch = (
        [pltpu.VMEM((n,) + piece, F32) for n in pieces for _ in range(NZ)]
        + [pltpu.VMEM((NZ - 1, n) + piece, F32) for n in pieces]
        + [pltpu.VMEM((NYC - 1, NZ, n) + piece, F32) for n in slots]
        + [pltpu.VMEM((NYC, NZ, n) + piece, F32) for n in slots]
        + [pltpu.VMEM((NYC * n, 8, HALF), F32) for n in part_slots for _ in range(NZ)]
        + [pltpu.VMEM((NYC, NZ, n, 8, HALF), F32) for n in part_slots]
        + [pltpu.VMEM((NZ - 1, n, 8, HALF), F32) for n in home_pieces]
        + [pltpu.VMEM((COLUMN,) + piece, F32) for _ in range(2)]
        + [
            pltpu.VMEM((2, COLUMN) + piece, F32),
            pltpu.VMEM((2, NX - 1, COLUMN) + piece, F32),
            pltpu.VMEM((2, COLUMN) + piece, F32),
            pltpu.VMEM((2, COLUMN) + piece, F32),
            pltpu.VMEM((COLUMN, HALF), F32),
            pltpu.VMEM((SLOTS, size, size), F32),
            pltpu.VMEM((SLOTS, size, size), BF16),
            pltpu.VMEM((SLOTS, size, size), BF16),
            pltpu.VMEM((SLOTS, size, size), F32),
            pltpu.VMEM((SLOTS, size, size), F32),
            pltpu.VMEM((NZ * cap, 8, HALF), F32),
            pltpu.VMEM((COLUMN, 8, HALF), F32),
            dma((2, NX - 1)), dma((2, NX - 1)),
            dma((3, NZ - 1)), dma((3, NZ - 1)),
            dma((3,)), dma((3,)),
            dma((2,)), dma((2, NZ)),
            dma((2, NZ - 1)), dma((2, NZ - 1)),
            dma((4,)), dma((5,)), dma((4,)),
        ]
    )
    halves = lambda a: a.reshape(-1, 4, 2, HALF).transpose(0, 2, 1, 3)
    whole = lambda a: a.reshape(COLUMN, 2, 4, HALF).transpose(0, 2, 1, 3).reshape(COLUMN, 4, size)
    new_w, new_m, new_left, new_right = pl.pallas_call(
        functools.partial(step_kernel, cap),
        out_shape=(
            jax.ShapeDtypeStruct((COLUMN, 8, HALF), F32),
            jax.ShapeDtypeStruct((COLUMN, 2) + piece, F32),
            jax.ShapeDtypeStruct((SLOTS, size, size), F32),
            jax.ShapeDtypeStruct((SLOTS, size, size), F32),
        ),
        in_specs=[pl.BlockSpec(memory_space=pltpu.SMEM)] + [vmem] * 2 + [hbm] * 7,
        out_specs=(vmem, any_spec, any_spec, any_spec),
        scratch_shapes=scratch,
        compiler_params=pltpu.CompilerParams(
            collective_id=1 + CAPS.index(cap), has_side_effects=True, vmem_limit_bytes=30 * 1024 * 1024
        ),
        name="step",
    )(
        table, mask, own_hot,
        halves(grads[0]), halves(moments), halves(weights).reshape(COLUMN, 8, HALF),
        left_stat[0, 0], right_stat[0, 0], left_root[0, 0], right_root[0, 0],
    )
    return whole(new_w), whole(new_m), new_left[None, None], new_right[None, None]


def on_device(grads, weights, moments, left_stat, right_stat, left_root, right_root, owner, extent):
    choice, table, mask, own_hot = make_plan(owner.reshape(1, COLUMN), extent.T)
    return lax.switch(
        choice[0, 0],
        [functools.partial(run_step, cap) for cap in CAPS],
        table, mask, own_hot, grads, moments, weights, left_stat, right_stat, left_root, right_root,
    )


def solution(mesh):
    in_specs = (
        P("tp", None, "fsdp", None),
        P("tp", "fsdp", None),
        P("tp", "fsdp", None),
        P("tp", "fsdp", None, None, None),
        P("tp", "fsdp", None, None, None),
        P("tp", "fsdp", None, None, None),
        P("tp", "fsdp", None, None, None),
        P("tp"),
        P("tp", None),
    )
    out_specs = (
        P("tp", "fsdp", None),
        P("tp", "fsdp", None),
        P("tp", "fsdp", None, None, None),
        P("tp", "fsdp", None, None, None),
    )
    return jax.shard_map(
        on_device, mesh=mesh, in_specs=in_specs, out_specs=out_specs, check_vma=False
    )
```

time: 113 us -> 105 us (0.929)
  Pallas kernels: 104 us -> 99.7 us
  local copies, waits for them, and re-layouts: 8.05 us -> 3.87 us
    pallas_call x1, Pallas kernels: 96.6 us -> 92.6 us  [run_step(): pl.pallas_call(functools.partial(step_kernel, cap), out_shape=(jax.ShapeD...]
    unnamed x6 -> x4, local copies, waits for them, and re-layouts: 6.85 us -> 3.87 us
    slice x1 -> x0, local copies, waits for them, and re-layouts: 1.2 us -> none  [on_device(): need[0, 0] <= CAPS[0]]
where the time goes in v4:
time: 105 us
  Pallas kernels  99.7 us (95%)
  local copies, waits for them, and re-layouts  3.87 us (4%)
  between operations  1.21 us (1%)
    pallas_call x1, Pallas kernels, run_step(): pl.pallas_call(functools.partial(step_kernel, cap), out_shape=(jax.ShapeD...  92.6 us
    pallas_call x1, Pallas kernels, make_plan(): pl.pallas_call(plan_kernel, out_shape=(jax.ShapeDtypeStruct((1, 1), jnp.i...  7.05 us
    unnamed x4, local copies, waits for them, and re-layouts  3.87 us

profile of v4, /device:TPU:1, one launch (start us, length us, event | category | flops | bytes accessed | tf_op | source)
XLA Modules:
  0.0 105.2 jit_solution(8625793815390871725)
XLA Ops:
  0.6 7.1 %plan.1 = (s32[1,1]{1,0:T(1,128)}, s32[8,384]{1,0:T(8,128)S(1)}, f32[2,128,128]{2,1,0:T(8,128)S(1)}, f32[8,128]{1,0:T(8,128)S(1)}) custom-call(s32[1,128]{1,0:T(1,128)} %bitcast.112, s32[2,128]{1,0:T(2,128)} %bitcast.111), custom_call_target="tpu_custom_call" | custom-call | tf_op jit(solution)/shard_map/plan/pallas_call | solution.py:378
  8.3 93.0 %conditional.1 = (f32[128,4,256]{2,1,0:T(4,128)S(1)}, f32[128,4,256]{2,1,0:T(4,128)S(1)}, f32[1,1,6,256,256]{4,3,2,1,0:T(8,128)S(1)}, f32[1,1,6,256,256]{4,3,2,1,0:T(8,128)S(1)}) conditional(s32[]{:T(128)} %bitcast.77, (f32[1,512,4,256]{3,2,1,0:T(4,128)}, f32[128,4,256]{2,1,0:T(4,128)}, f32[128,4,256]{2,1,0:T(4,128)}, ...), branch_computations={%region_0.0_spmd, %region_1.0_spmd, %region_2.0_spmd} | conditional | bytes 32 | solution.py:514
  8.5 92.6 %step.4 = (f32[128,8,128]{2,1,0:T(8,128)S(1)}, f32[128,2,4,128]{3,2,1,0:T(4,128)S(1)}, f32[6,256,256]{2,1,0:T(8,128)S(1)}, f32[6,256,256]{2,1,0:T(8,128)S(1)}) custom-call(s32[8,384]{1,0:T(8,128)S(1)} %get-tuple-element.74.table, f32[2,128,128]{2,1,0:T(8,128)S(1)} %get-tuple-element.75.mask, f32[8,128]{1,0:T(8,128)S(1)} %get-tuple-element.76.own_hot, ...), custom_call_target="tpu_custom_call" | custom-call | tf_op jit(solution)/shard_map/cond/branch_1_fun/step/pallas_call | solution.py:489
  101.3 0.8 copy.44
  102.1 0.8 copy.45
  102.9 1.1 %copy.46 = f32[1,1,6,256,256]{4,3,2,1,0:T(8,128)} copy(f32[1,1,6,256,256]{4,3,2,1,0:T(8,128)S(1)} %get-tuple-element.136) | data formatting | bytes 3145728
  104.0 1.1 %copy.47 = f32[1,1,6,256,256]{4,3,2,1,0:T(8,128)} copy(f32[1,1,6,256,256]{4,3,2,1,0:T(8,128)S(1)} %get-tuple-element.137) | data formatting | bytes 3145728

commit v5 on v4

--- a/solution.py
+++ b/solution.py
@@ -225,7 +225,7 @@
     def precondition(p, adam_row):
         first, last = PARTS[p]
 
-        @pl.loop(first, last)
+        @pl.loop(first, last, unroll=True)
         def _(j):
             high, low = split(gfull[j])
             inner = dot(lroot[j], high) + dot(lroot[j], low)

time: 105 us -> 101 us (0.962)
  Pallas kernels: 99.7 us -> 95.5 us
    pallas_call x1, Pallas kernels: 92.6 us -> 88.5 us  [run_step(): pl.pallas_call(functools.partial(step_kernel, cap), out_shape=(jax.ShapeD...]
where the time goes in v5:
time: 101 us
  Pallas kernels  95.5 us (95%)
  local copies, waits for them, and re-layouts  3.87 us (4%)
  between operations  1.21 us (1%)
    pallas_call x1, Pallas kernels, run_step(): pl.pallas_call(functools.partial(step_kernel, cap), out_shape=(jax.ShapeD...  88.5 us
    pallas_call x1, Pallas kernels, make_plan(): pl.pallas_call(plan_kernel, out_shape=(jax.ShapeDtypeStruct((1, 1), jnp.i...  7.05 us
    unnamed x4, local copies, waits for them, and re-layouts  3.87 us

profile of v5, /device:TPU:1, one launch (start us, length us, event | category | flops | bytes accessed | tf_op | source)
XLA Modules:
  0.0 100.8 jit_solution(10515142744497817279)
XLA Ops:
  0.6 7.1 %plan.1 = (s32[1,1]{1,0:T(1,128)}, s32[8,384]{1,0:T(8,128)S(1)}, f32[2,128,128]{2,1,0:T(8,128)S(1)}, f32[8,128]{1,0:T(8,128)S(1)}) custom-call(s32[1,128]{1,0:T(1,128)} %bitcast.112, s32[2,128]{1,0:T(2,128)} %bitcast.111), custom_call_target="tpu_custom_call" | custom-call | tf_op jit(solution)/shard_map/plan/pallas_call | solution.py:378
  8.3 88.7 %conditional.1 = (f32[128,4,256]{2,1,0:T(4,128)S(1)}, f32[128,4,256]{2,1,0:T(4,128)S(1)}, f32[1,1,6,256,256]{4,3,2,1,0:T(8,128)S(1)}, f32[1,1,6,256,256]{4,3,2,1,0:T(8,128)S(1)}) conditional(s32[]{:T(128)} %bitcast.77, (f32[1,512,4,256]{3,2,1,0:T(4,128)}, f32[128,4,256]{2,1,0:T(4,128)}, f32[128,4,256]{2,1,0:T(4,128)}, ...), branch_computations={%region_0.0_spmd, %region_1.0_spmd, %region_2.0_spmd} | conditional | bytes 32 | solution.py:514
  8.3 88.5 %step.3 = (f32[128,8,128]{2,1,0:T(8,128)S(1)}, f32[128,2,4,128]{3,2,1,0:T(4,128)S(1)}, f32[6,256,256]{2,1,0:T(8,128)S(1)}, f32[6,256,256]{2,1,0:T(8,128)S(1)}) custom-call(s32[8,384]{1,0:T(8,128)S(1)} %get-tuple-element.60.table, f32[2,128,128]{2,1,0:T(8,128)S(1)} %get-tuple-element.61.mask, f32[8,128]{1,0:T(8,128)S(1)} %get-tuple-element.62.own_hot, ...), custom_call_target="tpu_custom_call" | custom-call | tf_op jit(solution)/shard_map/cond/branch_0_fun/step/pallas_call | solution.py:489
  97.0 0.8 copy.44
  97.8 0.8 copy.45
  98.6 1.1 %copy.46 = f32[1,1,6,256,256]{4,3,2,1,0:T(8,128)} copy(f32[1,1,6,256,256]{4,3,2,1,0:T(8,128)S(1)} %get-tuple-element.136) | data formatting | bytes 3145728
  99.7 1.1 %copy.47 = f32[1,1,6,256,256]{4,3,2,1,0:T(8,128)} copy(f32[1,1,6,256,256]{4,3,2,1,0:T(8,128)S(1)} %get-tuple-element.137) | data formatting | bytes 3145728
